TPU v7x, 256 devices: a whole 4x4x8 slice. The times are simulated.
256 devices in a mesh: space: 32 (over z, y_lo, core), tm: 4 (over x), cores: 2 (over y_hi).
Axes of the slice: x: 4, y: 4 (y_hi: 2, y_lo: 2; y = y_hi * 2 + y_lo), z: 8, core: 2. Of those that a mesh axis runs over, the one named last changes fastest.
Arguments:
- initial_state: float32 [1024, 64, 512], P('space', 'cores'), may hold values from -6 to 6
- heat_source: float32 [1024, 64, 512], P('space', 'cores'), may hold values from -3 to 3
- source_amplitude: float32 [32], P('tm'), may hold values from 0.5 to 1.5
- diffusivity: float32 [32], P('space'), may hold values from 0.5 to 2
- robin_param: float32 [32], P('space'), may hold values from 0.5 to 4
- spectrum_x: float32 [32], replicated, may hold values from 0.002 to 0.38
- spectrum_y: float32 [64], P('cores'), may hold values from 0.002 to 0.38
- spectrum_z: float32 [512], replicated, may hold values from 0.002 to 0.38
- robin_in: float32 [32, 2, 32, 64, 512], P('space', None, 'tm', 'cores'), may hold values from -8 to 8
- open_flag: int32 [32, 64], P(None, 'cores'), may hold values from 0 to 1, as said below
- owner_side: int32 [32, 64], P(None, 'cores'), may hold values from 0 to 1, as said below
Outputs:
- robin_out: float32 [32, 2, 32, 64, 512], P('space', None, 'tm', 'cores')
- window_end: float32 [4, 1024, 64, 512], P('tm', 'space', 'cores')
Inputs may be any that keep to these rules, and one draw needn't show every extreme that they name: In each aligned group of 4 modes b of an interface exactly one has open_flag 0. In each aligned pair of modes b of an interface exactly one has owner_side 1.
All inputs are finite; a program needn't handle non-finite values.
Results may differ from a plain program's by a relative error of at most 0.00015.
Values sent between devices are 32-bit elements; how exact they have to be, the bound alone decides.
A program may use at most 128 MiB of HBM per device.

v0:
```python
import jax
import jax.numpy as jnp
from jax import lax
from jax.sharding import PartitionSpec as P

HIGHEST = lax.Precision.HIGHEST


def passed_along(block, axis, distance):
    devices = range(lax.axis_size(axis))
    route = [(i - distance, i) for i in devices if i - distance in devices]
    return lax.ppermute(block, axis, route)


def passed_along_2(x, axis, by):
    devices = lax.axis_size(axis)
    return lax.ppermute(x, axis, [(i, (i + by) % devices) for i in range(devices)])


def cosine_basis(order):
    mode_rows = jnp.arange(order, dtype=jnp.float32)[:, None]
    node_cols = jnp.arange(order, dtype=jnp.float32)[None, :]
    scaling = jnp.where(mode_rows == 0, jnp.sqrt(1.0 / order), jnp.sqrt(2.0 / order))
    return scaling * jnp.cos(jnp.pi * mode_rows * (node_cols + 0.5) / order)


def local(
    initial_state,
    heat_source,
    source_amplitude,
    diffusivity,
    robin_param,
    spectrum_x,
    spectrum_y,
    spectrum_z,
    robin_in,
    open_flag,
    owner_side,
):
    nodes_x, half_y, nodes_z = initial_state.shape
    nodes_y = half_y * lax.axis_size("cores")
    core_index = lax.axis_index("cores")
    basis_x = cosine_basis(nodes_x)
    basis_y = cosine_basis(nodes_y)
    basis_z = cosine_basis(nodes_z)
    mode_block = lax.dynamic_slice_in_dim(basis_y, core_index * half_y, half_y, 0)
    node_block = lax.dynamic_slice_in_dim(basis_y, core_index * half_y, half_y, 1)

    def local_forward(values):
        values = jnp.einsum("ax,xyz->ayz", basis_x, values, precision=HIGHEST)
        return jnp.einsum("cz,ayz->ayc", basis_z, values, precision=HIGHEST)

    pieces = (
        lax.all_gather(local_forward(initial_state), "cores", axis=1, tiled=True),
        lax.all_gather(local_forward(heat_source), "cores", axis=1, tiled=True),
    )
    start_modes, source_modes = tuple(
        (
            jnp.einsum("by,ayc->abc", mode_block, piece_part, precision=HIGHEST)
            for piece_part in pieces
        )
    )
    rates = spectrum_x[:, None, None] + spectrum_y[None, :, None] + spectrum_z[None, None, :]
    factor = 1.0 / (1.0 + diffusivity[0] * rates)
    edge_rows = jnp.stack(
        [
            basis_x[:, 0],
            basis_x[:, 1] - basis_x[:, 0],
            basis_x[:, nodes_x - 1],
            basis_x[:, nodes_x - 1] - basis_x[:, nodes_x - 2],
        ]
    )
    left_col = basis_x[:, 0][:, None, None]
    right_col = basis_x[:, nodes_x - 1][:, None, None]
    robin_here = robin_in[0]
    steps_here = source_amplitude.shape[0]
    windows = lax.axis_size("tm")
    tm_index = lax.axis_index("tm")
    opening = start_modes
    for window in range(windows):
        current = opening
        collected = []
        for substep in range(steps_here):
            forcing = current
            forcing = forcing + source_amplitude[substep] * source_modes
            forcing = (
                forcing
                + left_col * robin_here[0, substep][None]
                + right_col * robin_here[1, substep][None]
            )
            current = forcing * factor
            collected.append(jnp.einsum("ka,abc->kbc", edge_rows, current, precision=HIGHEST))
        closing = current
        traces = jnp.stack(collected)
        if window + 1 < windows:
            passed = passed_along(closing, "tm", 1)
            opening = jnp.where(tm_index == 0, start_modes, passed)
    subdomains = lax.axis_size("space")
    space_index = lax.axis_index("space")
    left_index = (space_index + subdomains - 1) % subdomains
    open_right = open_flag[space_index].astype(jnp.float32)[:, None]
    open_left = open_flag[left_index].astype(jnp.float32)[:, None]
    side_right = owner_side[space_index][:, None]
    side_left = owner_side[left_index][:, None]
    owns_right = side_right == 0
    owns_left = side_left == 1
    left_face = traces[:, 0:2]
    right_face = traces[:, 2:4]
    send_left = jnp.where(side_left == 0, left_face, 0.0)
    send_right = jnp.where(side_right == 1, right_face, 0.0)
    got_right = passed_along_2(send_left, "space", -1)
    got_left = passed_along_2(send_right, "space", 1)
    own_right_data = open_right * (got_right[:, 1] + robin_param[0] * got_right[:, 0])
    own_left_data = open_left * (robin_param[0] * got_left[:, 0] - got_left[:, 1])
    back_right = jnp.where(
        owns_right, open_right * (robin_param[0] * right_face[:, 0] - right_face[:, 1]), 0.0
    )
    back_left = jnp.where(
        owns_left, open_left * (left_face[:, 1] + robin_param[0] * left_face[:, 0]), 0.0
    )
    returned_left = passed_along_2(back_right, "space", 1)
    returned_right = passed_along_2(back_left, "space", -1)
    left_data = jnp.where(owns_left, own_left_data, returned_left)
    right_data = jnp.where(owns_right, own_right_data, returned_right)
    robin_out = jnp.stack([left_data, right_data])[None]
    spectral = jnp.einsum("ax,abc->xbc", basis_x, closing, precision=HIGHEST)
    spectral = jnp.einsum("cz,xbc->xbz", basis_z, spectral, precision=HIGHEST)
    physical = jnp.einsum(
        "by,xbz->xyz",
        node_block,
        lax.all_gather(spectral, "cores", axis=1, tiled=True),
        precision=HIGHEST,
    )
    return (robin_out, physical[None])


def solution(mesh):
    placed = (
        P("space", "cores", None),
        P("space", "cores", None),
        P("tm"),
        P("space"),
        P("space"),
        P(),
        P("cores"),
        P(),
        P("space", None, "tm", "cores", None),
        P(None, "cores"),
        P(None, "cores"),
    )
    return jax.shard_map(
        local,
        mesh=mesh,
        in_specs=placed,
        out_specs=(P("space", None, "tm", "cores", None), P("tm", "space", "cores", None)),
        check_vma=False,
    )
```

profile of v0, /device:TPU:3, one launch (start us, length us, event | category | flops | bytes accessed | tf_op | source)
XLA Modules:
  0.0 476.9 jit_solution(9938863236364807262)
XLA Ops:
  7.3 1.5 copy-done
  8.8 3.1 fusion.57
  11.9 10.7 %fusion.55 = f32[32,32,512]{2,1,0:T(8,128)} fusion(f32[32,32,512]{2,0,1:T(8,128)S(1)} %fusion.57, f32[512]{0:T(512)S(1)} %get-tuple-element.57, f32[512]{0:T(512)S(1)} %get-tuple-element.58, f32[512]{0:T(512)S(1)} %fusion.181), kind=kOutput, calls=%fused_computation.133 | convolution fusion | flops 3222011904 | bytes 4200448 | tf_op jit(solution)/shard_map/cz,ayz->ayc/dot_general | solution.py:51
  22.6 0.3 all-gather.4.cloned.1.call-start
  23.0 4.7 fusion.61
  27.6 10.7 %fusion.59 = f32[32,32,512]{2,1,0:T(8,128)} fusion(f32[32,32,512]{2,0,1:T(8,128)S(1)} %fusion.61, f32[512]{0:T(512)S(1)} %get-tuple-element.57, f32[512]{0:T(512)S(1)} %get-tuple-element.58, f32[512]{0:T(512)S(1)} %fusion.181), kind=kOutput, calls=%fused_computation.137 | convolution fusion | flops 3222011904 | bytes 4200448 | tf_op jit(solution)/shard_map/cz,ayz->ayc/dot_general | solution.py:51
  38.4 0.6 all-gather.8.cloned.1.call-start
  39.6 0.7 fusion.206
  40.6 0.2 cosine_multiply_fusion.4
  40.9 48.2 %all-gather.6.cloned.1.call-done = f32[32,64,512]{2,1,0:T(8,128)} async-done(((f32[32,32,512]{2,1,0:T(8,128)}), f32[32,64,512]{2,1,0:T(8,128)}) %all-gather.6.cloned.1.call-update) | async-done | bytes 4194320 | tf_op jit(solution)/shard_map/all_gather | solution.py:55
  89.1 4.2 fusion.160
  93.2 60.5 %all-gather.4.cloned.1.call-done = f32[32,64,512]{2,1,0:T(8,128)} async-done(((f32[32,32,512]{2,1,0:T(8,128)}), f32[32,64,512]{2,1,0:T(8,128)}) %all-gather.4.cloned.1.call-update) | async-done | bytes 4194320 | tf_op jit(solution)/shard_map/all_gather | solution.py:54
  153.7 14.2 %fusion.49 = (f32[32,32,512]{2,1,0:T(8,128)}, f32[32,512,32]{1,2,0:T(8,128)}) fusion(f32[32,512,32]{1,2,0:T(8,128)S(1)} %fusion.160, f32[32,512]{1,0:T(8,128)S(1)} %get-tuple-element.16, f32[32,512]{1,0:T(8,128)S(1)} %get-tuple-element.17, f32[]{:T(128)} %bitcast.45, f32[32,512]{1,0:T(8,128)S(1)} %get-tuple-element.18, ...), kind=kOutput, calls=%fused_computation.113 | convolution fusion | flops 434110464 | bytes 11570216 | tf_op jit(solution)/shard_map/by,ayc->abc/dot_general | solution.py:59
  167.9 3.1 collective-permute-start
  171.0 45.6 %collective-permute-done = f32[32,32,512]{2,1,0:T(8,128)} collective-permute-done((f32[32,32,512]{2,1,0:T(8,128)}, f32[32,32,512]{2,1,0:T(8,128)}, u32[]{:S(2)}, u32[]{:S(2)}) %collective-permute-start) | collective-permute-done | bytes 2097184 | tf_op jit(solution)/shard_map/ppermute | solution.py:12
  216.6 11.1 %fusion.50 = f32[32,32,512]{2,1,0:T(8,128)S(1)} fusion(f32[32,32,512]{2,1,0:T(8,128)} %collective-permute-done, f32[32,512,32]{1,2,0:T(8,128)} %get-tuple-element.54, f32[32,512,32]{1,2,0:T(8,128)S(1)} %fusion.160, f32[32,512]{1,0:T(8,128)S(1)} %get-tuple-element.16, f32[32,512]{1,0:T(8,128)S(1)} %get-tuple-element.17, f32[]{:T(128)} %bitcast.45, ...), kind=kLoop, calls=%fused_computation.114 | loop fusion | flops 31981568 | bytes 9443621 | tf_op jit(solution)/shard_map/mul | solution.py:91
  227.7 3.1 collective-permute-start.1
  230.8 44.4 %collective-permute-done.1 = f32[32,32,512]{2,1,0:T(8,128)S(1)} collective-permute-done((f32[32,32,512]{2,1,0:T(8,128)S(1)}, f32[32,32,512]{2,1,0:T(8,128)S(1)}, u32[]{:S(2)}, u32[]{:S(2)}) %collective-permute-start.1) | collective-permute-done | bytes 2097184 | tf_op jit(solution)/shard_map/ppermute | solution.py:12
  275.2 10.5 %fusion.51 = f32[32,32,512]{2,1,0:T(8,128)} fusion(f32[32,32,512]{2,1,0:T(8,128)S(1)} %collective-permute-done.1, f32[32,512,32]{1,2,0:T(8,128)S(1)} %copy-done.4, f32[32,512,32]{1,2,0:T(8,128)S(1)} %fusion.160, f32[32,512]{1,0:T(8,128)S(1)} %get-tuple-element.16, f32[32,512]{1,0:T(8,128)S(1)} %get-tuple-element.17, f32[]{:T(128)} %bitcast.45, ...), kind=kLoop, calls=%fused_computation.115 | loop fusion | flops 31981568 | bytes 9443621 | tf_op jit(solution)/shard_map/mul | solution.py:91
  285.7 3.1 collective-permute-start.2
  289.4 0.8 fusion.188
  290.2 0.8 compare_bitcast_fusion.2
  291.0 41.6 %collective-permute-done.2 = f32[32,32,512]{2,1,0:T(8,128)} collective-permute-done((f32[32,32,512]{2,1,0:T(8,128)}, f32[32,32,512]{2,1,0:T(8,128)}, u32[]{:S(2)}, u32[]{:S(2)}) %collective-permute-start.2) | collective-permute-done | bytes 2097184 | tf_op jit(solution)/shard_map/ppermute | solution.py:12
  332.5 14.2 %fusion.52 = (f32[32,32,512]{2,1,0:T(8,128)S(1)}, f32[32,32,512]{2,1,0:T(8,128)}, f32[32,32,512]{2,1,0:T(8,128)}, f32[32,32,512]{2,1,0:T(8,128)}, f32[32,32,512]...) fusion(f32[32,512,32]{1,2,0:T(8,128)S(1)} %fusion.160, ...), kind=kLoop, calls=%fused_computation.116 | loop fusion | flops 31981568 | bytes 24123684 | tf_op jit(solution)/shard_map/mul | solution.py:91
  346.8 3.1 fusion.77
  349.9 9.4 %fusion.53 = f32[32,32,512]{2,1,0:T(8,128)} fusion(f32[32,32,512]{2,0,1:T(8,128)S(1)} %fusion.77, f32[512]{0:T(512)S(1)} %get-tuple-element.57, f32[512]{0:T(512)S(1)} %get-tuple-element.58, f32[512]{0:T(512)S(1)} %fusion.181), kind=kOutput, calls=%fused_computation.131 | convolution fusion | flops 3222011904 | bytes 4200448 | tf_op jit(solution)/shard_map/cz,xbc->xbz/dot_general | solution.py:127
  359.4 4.1 fusion.90
  363.5 2.3 fusion.96
  365.8 2.3 fusion.102
  368.1 2.3 fusion.108
  370.5 2.3 fusion.114
  372.8 2.7 fusion.120
  375.5 2.3 fusion.126
  377.8 2.3 fusion.84
  380.1 1.0 fusion.204
  381.1 0.3 copy_select_fusion.1
  381.4 3.7 collective-permute-start.3
  385.1 1.3 fusion.205
  386.4 0.2 fusion.144
  386.7 0.3 copy_select_fusion
  387.0 0.6 collective-permute-start.5
  387.5 65.4 %collective-permute-done.4 = f32[8,32,512]{2,1,0:T(8,128)S(1)} collective-permute-done((f32[8,32,512]{2,1,0:T(8,128)S(1)}, f32[8,32,512]{2,1,0:T(8,128)S(1)}, u32[]{:S(2)}, u32[]{:S(2)}) %collective-permute-start.4) | collective-permute-done | bytes 524320 | tf_op jit(solution)/shard_map/ppermute | solution.py:17
  453.0 0.3 fusion.141
  453.3 0.3 collective-permute-start.6
  453.6 9.3 %collective-permute-done.6 = f32[8,32,512]{2,1,0:T(8,128)S(1)} collective-permute-done((f32[8,32,512]{2,1,0:T(8,128)S(1)}, f32[8,32,512]{2,1,0:T(8,128)S(1)}, u32[]{:S(2)}, u32[]{:S(2)}) %collective-permute-start.6) | collective-permute-done | bytes 524320 | tf_op jit(solution)/shard_map/ppermute | solution.py:17
  462.9 0.2 fusion.137
  463.1 1.1 maximum_bitcast_fusion
  464.2 6.0 %convolution_bitcast_fusion = f32[1,32,32,512]{3,2,1,0:T(8,128)} fusion(f32[32,64,512]{2,1,0:T(8,128)} %all-gather.8.cloned.1.call-done, f32[64,64]{1,0:T(8,128)S(1)} %cosine_multiply_fusion.4, s32[]{:T(128)S(6)} %select_n.140), kind=kOutput, calls=%fused_computation.160 | convolution fusion | flops 402653184 | bytes 6307844 | tf_op jit(solution)/shard_map/by,xbz->xyz/dot_general | solution.py:128
  (50 shorter events, 0.6 us)
Async XLA Ops:
  7.2 1.6 copy-start
  7.2 81.9 %all-gather.6.cloned.1.call-start = ((), (), s32[]{:S(2)}) async-start(), calls=%async_computation.1 | async-start | bytes 6291456 | tf_op jit(solution)/shard_map/all_gather | solution.py:55
  22.6 131.1 %all-gather.4.cloned.1.call-start = ((), (), s32[]{:S(2)}) async-start(), calls=%async_computation | async-start | bytes 6291456 | tf_op jit(solution)/shard_map/all_gather | solution.py:54
  38.3 1.3 copy-start.12
  38.3 2.1 copy-start.14
  38.3 2.1 copy-start.15
  38.3 2.4 copy-start.11
  38.4 425.8 %all-gather.8.cloned.1.call-start = ((), (), s32[]{:S(2)}) async-start(), calls=%async_computation.2 | async-start | bytes 6291456 | tf_op jit(solution)/shard_map/all_gather | solution.py:131
  40.9 112.9 %copy-start.13 = (f32[512]{0:T(512)S(1)}, f32[512]{0:T(512)}, u32[]{:S(2)}) copy-start(f32[512]{0:T(512)} %param.18) | copy-start | bytes 6148
  167.9 48.7 %collective-permute-start = (f32[32,32,512]{2,1,0:T(8,128)}, f32[32,32,512]{2,1,0:T(8,128)}, u32[]{:S(2)}, u32[]{:S(2)}) collective-permute-start(f32[32,32,512]{2,1,0:T(8,128)} %get-tuple-element.53), channel_id=1, source_target_pairs={{0,2},{2,4},{4,6},{1,3},{3,5},{5,7},{8,10},{10,12},{12,14},{9,11},... | collective-permute-start | bytes 6291464 | tf_op jit(solution)/shard_map/ppermute | solution.py:12
  216.6 58.6 %copy-start.4 = (f32[32,512,32]{1,2,0:T(8,128)S(1)}, f32[32,512,32]{1,2,0:T(8,128)}, u32[]{:S(2)}) copy-start(f32[32,512,32]{1,2,0:T(8,128)} %get-tuple-element.54) | copy-start | bytes 6291460
  227.7 47.5 %collective-permute-start.1 = (f32[32,32,512]{2,1,0:T(8,128)S(1)}, f32[32,32,512]{2,1,0:T(8,128)S(1)}, u32[]{:S(2)}, u32[]{:S(2)}) collective-permute-start(f32[32,32,512]{2,1,0:T(8,128)S(1)} %fusion.50), channel_id=1, source_target_pairs={{0,2},{2,4},{4,6},{1,3},{3,5},{5,7},{8,10},{10,12},{12,14},{9,11},... | collective-permute-start | bytes 6291464 | tf_op jit(solution)/shard_map/ppermute | solution.py:12
  285.7 46.9 %collective-permute-start.2 = (f32[32,32,512]{2,1,0:T(8,128)}, f32[32,32,512]{2,1,0:T(8,128)}, u32[]{:S(2)}, u32[]{:S(2)}) collective-permute-start(f32[32,32,512]{2,1,0:T(8,128)} %fusion.51), channel_id=1, source_target_pairs={{0,2},{2,4},{4,6},{1,3},{3,5},{5,7},{8,10},{10,12},{12,14},{9,11},... | collective-permute-start | bytes 6291464 | tf_op jit(solution)/shard_map/ppermute | solution.py:12
  346.7 3.1 copy-start.2
  359.3 4.2 copy-start.10
  359.3 6.5 %copy-start.9 = (f32[32,32,512]{2,1,0:T(8,128)S(1)}, f32[32,32,512]{2,1,0:T(8,128)}, u32[]{:S(2)}) copy-start(f32[32,32,512]{2,1,0:T(8,128)} %get-tuple-element.7) | copy-start | bytes 6291460
  363.5 4.6 copy-start.8
  365.8 4.6 copy-start.7
  368.1 4.6 copy-start.6
  370.5 5.0 %copy-start.5 = (f32[32,32,512]{2,1,0:T(8,128)S(1)}, f32[32,32,512]{2,1,0:T(8,128)}, u32[]{:S(2)}) copy-start(f32[32,32,512]{2,1,0:T(8,128)} %get-tuple-element.3) | copy-start | bytes 6291460
  372.8 5.0 %copy-start.3 = (f32[32,32,512]{2,1,0:T(8,128)S(1)}, f32[32,32,512]{2,1,0:T(8,128)}, u32[]{:S(2)}) copy-start(f32[32,32,512]{2,1,0:T(8,128)} %copy-done.2) | copy-start | bytes 6291460
  381.4 71.5 %collective-permute-start.3 = (f32[8,2,32,512]{3,2,0,1:T(8,128)S(1)}, f32[8,2,32,512]{3,2,0,1:T(8,128)S(1)}, u32[]{:S(2)}, u32[]{:S(2)}) collective-permute-start(f32[8,2,32,512]{3,2,0,1:T(8,128)S(1)} %copy_select_fusion.1), channel_id=1, source_target_pairs={{0,8},{8,16},{16,24},{24,32},{32,40},{40,48},{48,56},{56,64},{64,7... | collective-permute-start | bytes 3145736 | tf_op jit(solution)/shard_map/ppermute | solution.py:17
  386.6 66.4 %collective-permute-start.4 = (f32[8,32,512]{2,1,0:T(8,128)S(1)}, f32[8,32,512]{2,1,0:T(8,128)S(1)}, u32[]{:S(2)}, u32[]{:S(2)}) collective-permute-start(f32[8,32,512]{2,1,0:T(8,128)S(1)} %fusion.144), channel_id=1, source_target_pairs={{0,8},{8,16},{16,24},{24,32},{32,40},{40,48},{48,56},{56,64},{64,7... | collective-permute-start | bytes 1572872 | tf_op jit(solution)/shard_map/ppermute | solution.py:17
  387.0 66.6 %collective-permute-start.5 = (f32[8,2,32,512]{3,2,0,1:T(8,128)S(1)}, f32[8,2,32,512]{3,2,0,1:T(8,128)S(1)}, u32[]{:S(2)}, u32[]{:S(2)}) collective-permute-start(f32[8,2,32,512]{3,2,0,1:T(8,128)S(1)} %copy_select_fusion), channel_id=1, source_target_pairs={{0,248},{8,0},{16,8},{24,16},{32,24},{40,32},{48,40},{56,48},{64,5... | collective-permute-start | bytes 3145736 | tf_op jit(solution)/shard_map/ppermute | solution.py:17
  453.3 9.6 %collective-permute-start.6 = (f32[8,32,512]{2,1,0:T(8,128)S(1)}, f32[8,32,512]{2,1,0:T(8,128)S(1)}, u32[]{:S(2)}, u32[]{:S(2)}) collective-permute-start(f32[8,32,512]{2,1,0:T(8,128)S(1)} %get-tuple-element.44), channel_id=1, source_target_pairs={{0,248},{8,0},{16,8},{24,16},{32,24},{40,32},{48,40},{56,48},{64,5... | collective-permute-start | bytes 1572872 | tf_op jit(solution)/shard_map/ppermute | solution.py:17
  463.1 7.1 %copy-start.1 = (f32[32,32,512]{2,1,0:T(8,128)S(1)}, f32[32,32,512]{2,1,0:T(8,128)}, u32[]{:S(2)}) copy-start(f32[32,32,512]{2,1,0:T(8,128)} %param.12) | copy-start | bytes 6291460
Sparse Core Ops, SparseCore 0:
  22.8 66.2 all-gather.5
  90.8 62.8 all-gather.3
  359.5 99.1 all-gather.7
where the time goes:
time: 484 us; the launch traced here: 477 us
  waiting for transfers between devices  315 us (65%)
  matrix products  86.7 us (18%)
  other arithmetic  41.4 us (9%)
  between operations  15.7 us (3%)
  starting transfers between devices  14.7 us (3%)
    ppermute x3, waiting for transfers between devices, passed_along(): return lax.ppermute(block, axis, route)  132 us
    ppermute x4, waiting for transfers between devices, passed_along_2(): lax.ppermute(x, axis, [(i, (i + by) % devices) for i in range(devices)])  74.8 us
    all_gather x1, waiting for transfers between devices, local(): lax.all_gather(local_forward(initial_state), 'cores', axis=1, tiled=True)  60.5 us
    all_gather x1, waiting for transfers between devices, local(): lax.all_gather(local_forward(heat_source), 'cores', axis=1, tiled=True)  48.2 us
    mul x3, other arithmetic, local(): current = forcing * factor  35.8 us
    dot_general x2, matrix products, local_forward(): return jnp.einsum('cz,ayz->ayc', basis_z, values, precision=HIGHEST)  21.4 us
    dot_general x8, matrix products, local(): jnp.einsum('ka,abc->kbc', edge_rows, current, precision=HIGHEST)  20.6 us
    dot_general x2, matrix products, local(): jnp.einsum('by,ayc->abc', mode_block, piece_part, precision=HIGHEST)  18.3 us
  transfers between devices with their start and end apart: 10, of which 7 were waited for; matrix products, arithmetic and copies ran while one was open for 10% of the time, Pallas kernels for 0%

commit v1 on v0

v1 whole, which is shorter than its diff:
```python
import functools

import jax
import jax.numpy as jnp
import ml_dtypes
import numpy as np
from jax import lax
from jax.experimental import pallas as pl
from jax.experimental.pallas import tpu as pltpu
from jax.sharding import PartitionSpec as P

MESH = pl.DeviceIdType.MESH
F32, BF16 = jnp.float32, jnp.bfloat16
NX, NY, NZ, STEPS, TM, SPACE = 32, 64, 512, 8, 4, 32
CB = NZ // TM
PERM = list(range(0, NX, 2)) + list(range(1, NX, 2))


def cosine(n):
    k = np.arange(n)[:, None]
    i = np.arange(n)[None, :]
    scale = np.where(k == 0, np.sqrt(1.0 / n), np.sqrt(2.0 / n))
    return scale * np.cos(np.pi * k * (i + 0.5) / n)


C_X, C_Y, C_Z = cosine(NX), cosine(NY), cosine(NZ)
EDGE = C_X[PERM, 0]
VALUE_W = [float(v) for v in EDGE * EDGE]
SLOPE_W = [float(v) for v in (C_X[PERM, 1] - C_X[PERM, 0]) * EDGE]


def split_constant(m):
    hi = np.asarray(m, np.float32).astype(ml_dtypes.bfloat16)
    lo = (np.asarray(m, np.float64) - hi.astype(np.float64)).astype(np.float32)
    return np.stack([hi, lo.astype(ml_dtypes.bfloat16)])


def constants():
    eye8, eye4 = np.eye(8), np.eye(4)
    x_fwd = np.kron(C_X[PERM] / EDGE[:, None], eye8)
    x_inv = np.kron((C_X[PERM] * EDGE[:, None]).T, eye8)
    cy = C_Y.reshape(8, 8, 8, 8)
    y_fwd = np.einsum("pbqy,ac->pabqcy", cy, eye4).reshape(256, 256)
    y_inv = np.einsum("pbqy,ac->qaypcb", cy, eye4).reshape(2, 128, 256)
    y_inv = np.stack([split_constant(y_inv[0]), split_constant(y_inv[1])])
    z_fwd = split_constant(C_Z.T)
    z_fwd = z_fwd.reshape(2, NZ, TM, CB).transpose(2, 1, 0, 3).reshape(TM, NZ, 2 * CB)
    z_inv = split_constant(C_Z).reshape(2, TM, CB, NZ)
    return (split_constant(x_fwd), split_constant(y_fwd), y_inv, split_constant(x_inv), z_fwd, z_inv)


def split(v):
    hi = v.astype(BF16)
    return hi, (v - hi.astype(F32)).astype(BF16)


def dot(a, b):
    return jnp.dot(a, b, preferred_element_type=F32)


def const_dot(m_hi, m_lo, v):
    hi, lo = split(v)
    return dot(m_hi, hi) + (dot(m_lo, hi) + dot(m_hi, lo))


def sweep_kernel(
    state_in, heat_in, robin_in, zf_in,
    amp_s, diff_s, param_s, specx_s, specy, specz, flag, owner,
    xf, yf, yi, xi, zi,
    robin_out, ends_out,
    xin, zf, v, sycol, ptile, amp, rb, modes, src, fac, tr, coef, ob, tbuf, ubuf, wr, acc,
    s_in, s_zf, s_rl, s_rs, r_rb, s_ro, s_f, r_f, s_y, r_y, s_p, r_p, s_a, r_a,
    s_o, r_o, s_w, r_w, s_out,
):
    s = lax.axis_index("space")
    w = lax.axis_index("tm")
    h = lax.axis_index("cores")
    oh = 1 - h
    left = lax.rem(s + SPACE - 1, SPACE)
    right = lax.rem(s + 1, SPACE)

    def remote(a, b, ss, rs, to):
        return pltpu.make_async_remote_copy(
            src_ref=a, dst_ref=b, send_sem=ss, recv_sem=rs, device_id=to, device_id_type=MESH
        )

    def other(d):
        return lax.rem(w + d, TM)

    ins = (state_in, heat_in)
    zf_copy = pltpu.make_async_copy(zf_in.at[w], zf, s_zf)
    zf_copy.start()

    def load(i, yt):
        rows = pl.ds(pl.multiple_of(yt * 8, 8), 8)
        return pltpu.make_async_copy(ins[i].at[:, rows, :], xin.at[i, :, rows, :], s_in.at[i, yt])

    for yt in range(4):
        for i in range(2):
            load(i, yt).start()

    def robin_block(d):
        return robin_in.at[0, :, :, :, pl.ds(pl.multiple_of(d * CB, CB), CB)]

    own_robin = pltpu.make_async_copy(robin_block(w), rb.at[h, w], s_rl)
    own_robin.start()

    barrier = pltpu.get_barrier_semaphore()
    for d in range(1, TM):
        pl.semaphore_signal(barrier, inc=1, device_id=(s, other(d), h), device_id_type=MESH)
    for d in range(TM):
        pl.semaphore_signal(barrier, inc=1, device_id=(s, other(d), oh), device_id_type=MESH)
        pl.semaphore_signal(barrier, inc=1, device_id=(left, other(d), h), device_id_type=MESH)
        pl.semaphore_signal(barrier, inc=1, device_id=(right, other(d), h), device_id_type=MESH)

    def column(row):
        n = row.shape[1]
        on = lax.broadcasted_iota(jnp.int32, (n, n), 0) == lax.broadcasted_iota(jnp.int32, (n, n), 1)
        picked = jnp.where(on, jnp.broadcast_to(row, (n, n)), 0.0)
        return jnp.broadcast_to(jnp.sum(picked, axis=1, keepdims=True), (n, CB))

    for j in range(STEPS):
        amp[w, j] = jnp.full((8, CB), amp_s[j], F32)
    ptile[1] = jnp.full((8, CB), param_s[0], F32)
    sycol[h] = column(specy[...])
    pl.semaphore_wait(barrier, 15)

    small = [
        remote(sycol.at[h], sycol.at[h], s_y, r_y, (s, w, oh)),
        remote(ptile.at[1], ptile.at[0], s_p.at[0], r_p.at[0], (right, w, h)),
        remote(ptile.at[1], ptile.at[2], s_p.at[1], r_p.at[1], (left, w, h)),
    ]
    for d in range(1, TM):
        small.append(remote(amp.at[w], amp.at[w], s_a.at[d], r_a.at[w], (s, other(d), h)))
    for c in small:
        c.start()
    same_half = []
    for d in range(1, TM):
        c = remote(robin_block(other(d)), rb.at[h, w], s_rs.at[d], r_rb.at[h, w], (s, other(d), h))
        c.start()
        same_half.append(c)

    def fwd_send(yt):
        return remote(v.at[h, yt], v.at[h, yt], s_f.at[yt], r_f.at[yt], (s, w, oh))

    zf_copy.wait()

    def fwd_chunk(yt, carry):
        rows = pl.ds(pl.multiple_of(yt * 8, 8), 8)
        zs = []
        for i in range(2):
            load(i, yt).wait()
            hi, lo = split(xin[i, :, rows, :].reshape(NX * 8, NZ))
            both = dot(hi, zf[...])
            zs.append(both[:, :CB] + (both[:, CB:] + dot(lo, zf[:, :CB])))
        res = const_dot(xf[0], xf[1], jnp.concatenate(zs, axis=1))
        v[h, yt, 0] = res[:, :CB].reshape(NX, 8, CB)
        v[h, yt, 1] = res[:, CB:].reshape(NX, 8, CB)
        fwd_send(yt).start()
        return carry

    lax.fori_loop(0, 4, fwd_chunk, 0)

    pl_copy = small
    for c in pl_copy[:3]:
        c.wait_send()
    remote(sycol.at[oh], sycol.at[oh], s_y, r_y, (s, w, oh)).wait_recv()
    small[1].wait_recv()
    small[2].wait_recv()

    def coefficient(at, here, beyond):
        opened = column(flag[pl.ds(at, 1), :].astype(F32))
        side = column(owner[pl.ds(at, 1), :].astype(F32))
        p = jnp.where(side > 0.5, beyond, here)
        return opened, opened * p

    pt = [jnp.broadcast_to(ptile[i][0:1], (32, CB)) for i in range(3)]
    o_l, op_l = coefficient(left, pt[0], pt[1])
    o_r, op_r = coefficient(s, pt[1], pt[2])
    coef[0] = o_l
    coef[1] = op_l
    coef[2] = o_r
    coef[3] = op_r

    sz = jnp.broadcast_to(specz[:, pl.ds(pl.multiple_of(w * CB, CB), CB)], (8, CB))

    def factor(bt, carry):
        sy = sycol[lax.div(bt, 4), pl.ds(pl.multiple_of(lax.rem(bt, 4) * 8, 8), 8), :]
        for a in range(NX):
            rate = (specx_s[PERM[a]] + sy) + sz
            fac[bt, a] = 1.0 / (1.0 + diff_s[0] * rate)
        return carry

    lax.fori_loop(0, 8, factor, 0)

    for yt in range(4):
        fwd_send(yt).wait_send()
    def cross(d):
        return remote(robin_block(other(d)), rb.at[h, w], s_ro.at[d], r_rb.at[h, w], (s, other(d), oh))

    for d in range(TM):
        cross(d).start()

    for yt in range(4):
        remote(v.at[oh, yt], v.at[oh, yt], s_f.at[yt], r_f.at[yt], (s, w, oh)).wait_recv()

    def y_forward(g, carry):
        at = pl.ds(g * 4, 4)
        rhs = jnp.concatenate([v[:, :, i, at].reshape(256, CB) for i in range(2)], axis=1)
        res = const_dot(yf[0], yf[1], rhs)
        modes[0, :, at] = res[:, :CB].reshape(8, 4, 8, CB)
        src[:, at] = res[:, CB:].reshape(8, 4, 8, CB)
        return carry

    lax.fori_loop(0, 8, y_forward, 0)

    own_robin.wait()
    for d in range(1, TM):
        f = other(d)
        remote(rb.at[h, f], rb.at[h, f], s_rs.at[d], r_rb.at[h, f], (s, f, h)).wait_recv()
        remote(amp.at[f], amp.at[f], s_a.at[d], r_a.at[f], (s, f, h)).wait_recv()

    def steps(k, half, bt, traces):
        tile = half * 4 + bt
        rows = pl.ds(pl.multiple_of(bt * 8, 8), 8)
        for g in range(4):
            a0 = g * 8
            mu = [modes[k, tile, a0 + i] for i in range(8)]
            fs = [fac[tile, a0 + i] for i in range(8)]
            sg = [src[tile, a0 + i] for i in range(8)]
            for j in range(STEPS):
                r0 = rb[half, k, 0, j, rows, :]
                r1 = rb[half, k, 1, j, rows, :]
                p = r0 + r1 if g < 2 else r0 - r1
                am = amp[k, j]
                for i in range(8):
                    mu[i] = (mu[i] + (am * sg[i] + p)) * fs[i]
                if traces:
                    val = [VALUE_W[a0 + i] * mu[i] for i in range(8)]
                    slo = [SLOPE_W[a0 + i] * mu[i] for i in range(8)]
                    val = sum(val[1:], val[0])
                    slo = sum(slo[1:], slo[0])
                    if g % 2 == 0:
                        tr[j, g] = val
                        tr[j, g + 1] = slo
                    elif g == 1:
                        tr[j, 0] += val
                        tr[j, 1] += slo
                    else:
                        e0, e1 = tr[j, 0], tr[j, 1]
                        o0 = tr[j, 2] + val
                        o1 = tr[j, 3] + slo
                        at = k * STEPS + j
                        ob[1, at, rows, :] = coef[0, rows, :] * (e1 + o1) + coef[1, rows, :] * (e0 + o0)
                        ob[0, at, rows, :] = coef[3, rows, :] * (e0 - o0) - coef[2, rows, :] * (o1 - e1)
            for i in range(8):
                modes[k + 1, tile, a0 + i] = mu[i]

    def own_steps(t, carry):
        k, bt = lax.div(t, 4), lax.rem(t, 4)
        steps(k, h, bt, True)
        return carry

    def robin_send(side, k):
        to = left if side == 1 else right
        return remote(
            ob.at[side, pl.ds(pl.multiple_of(k * STEPS, STEPS), STEPS)],
            robin_out.at[0, side, :, :, pl.ds(pl.multiple_of(w * CB, CB), CB)],
            s_o.at[side, k], r_o.at[side, w], (to, k, h),
        )

    def own_window(k, carry):
        lax.fori_loop(k * 4, k * 4 + 4, own_steps, 0)
        robin_send(0, k).start()
        robin_send(1, k).start()
        return carry

    lax.fori_loop(0, TM, own_window, 0)

    def end_send(k):
        return remote(ubuf.at[k], wr.at[w], s_w.at[k], r_w.at[w], (s, k, h))

    def other_window(k, carry):
        remote(rb.at[oh, k], rb.at[oh, k], s_ro.at[0], r_rb.at[oh, k], (s, k, oh)).wait_recv()

        def body(bt, c):
            steps(k, oh, bt, False)
            return c

        lax.fori_loop(0, 4, body, 0)
        my_hi, my_lo = yi[h, 0], yi[h, 1]

        def y_inverse(g, c):
            a, b = pl.ds(g * 8, 4), pl.ds(g * 8 + 4, 4)
            rhs = jnp.concatenate(
                [modes[k + 1, :, a].reshape(256, CB), modes[k + 1, :, b].reshape(256, CB)], axis=1
            )
            res = const_dot(my_hi, my_lo, rhs)
            tbuf[:, a] = res[:, :CB].reshape(4, 4, 8, CB)
            tbuf[:, b] = res[:, CB:].reshape(4, 4, 8, CB)
            return c

        lax.fori_loop(0, 4, y_inverse, 0)

        def x_inverse(q, c):
            rhs = jnp.concatenate(
                [tbuf[2 * q].reshape(256, CB), tbuf[2 * q + 1].reshape(256, CB)], axis=1
            )
            res = const_dot(xi[0], xi[1], rhs)
            ubuf[k, 2 * q] = res[:, :CB].reshape(NX, 8, CB)
            ubuf[k, 2 * q + 1] = res[:, CB:].reshape(NX, 8, CB)
            return c

        lax.fori_loop(0, 2, x_inverse, 0)

        @pl.when(k != w)
        def _():
            end_send(k).start()

        return carry

    lax.fori_loop(0, TM, other_window, 0)

    def z_inverse(ref, index, b, first):
        def body(yt, c):
            hi, lo = split(ref[index, yt].reshape(NX * 8, CB))
            m_hi, m_lo = zi[0, b], zi[1, b]
            part = (dot(hi, m_hi) + (dot(lo, m_hi) + dot(hi, m_lo))).reshape(NX, 8, NZ)
            if first:
                acc[yt] = part
            else:
                acc[yt] += part
            return c

        lax.fori_loop(0, 4, body, 0)

    z_inverse(ubuf, w, w, True)
    for d in (1, 3, 2):
        f = other(d)
        remote(ubuf.at[f], wr.at[f], s_w.at[f], r_w.at[f], (s, f, h)).wait_recv()
        z_inverse(wr, f, f, False)

    def store(yt):
        rows = pl.ds(pl.multiple_of(yt * 8, 8), 8)
        return pltpu.make_async_copy(acc.at[yt], ends_out.at[0, :, rows, :], s_out.at[yt])

    for yt in range(4):
        store(yt).start()

    for c in small[3:]:
        c.wait_send()
    for c in same_half:
        c.wait_send()
    for d in range(TM):
        cross(d).wait_send()
    for k in range(TM):
        for side in range(2):
            robin_send(side, k).wait_send()
    for d in range(1, TM):
        end_send(other(d)).wait_send()
    for k in range(TM):
        for side in range(2):
            remote(
                ob.at[side, pl.ds(k * STEPS, STEPS)],
                robin_out.at[0, side, :, :, pl.ds(k * CB, CB)],
                s_o.at[side, k], r_o.at[side, k], (left, k, h),
            ).wait_recv()
    for yt in range(4):
        store(yt).wait()


def local(
    initial_state, heat_source, source_amplitude, diffusivity, robin_param,
    spectrum_x, spectrum_y, spectrum_z, robin_in, open_flag, owner_side,
):
    xf, yf, yi, xi, zf, zi = (jnp.asarray(c) for c in constants())
    any_spec = pl.BlockSpec(memory_space=pl.ANY)
    smem = pl.BlockSpec(memory_space=pltpu.SMEM)
    vmem = pl.BlockSpec(memory_space=pltpu.VMEM)
    dma = pltpu.SemaphoreType.DMA
    tile = (8, CB)
    return pl.pallas_call(
        sweep_kernel,
        out_shape=(
            jax.ShapeDtypeStruct((1, 2, STEPS, 32, NZ), F32),
            jax.ShapeDtypeStruct((1, NX, 32, NZ), F32),
        ),
        in_specs=[any_spec] * 4 + [smem] * 4 + [vmem] * 9,
        out_specs=(any_spec, any_spec),
        scratch_shapes=[
            pltpu.VMEM((2, NX, 32, NZ), F32),
            pltpu.VMEM((NZ, 2 * CB), BF16),
            pltpu.VMEM((2, 4, 2, NX) + tile, F32),
            pltpu.VMEM((2, 32, CB), F32),
            pltpu.VMEM((3,) + tile, F32),
            pltpu.VMEM((TM, STEPS) + tile, F32),
            pltpu.VMEM((2, TM, 2, STEPS, 32, CB), F32),
            pltpu.VMEM((TM + 1, 8, NX) + tile, F32),
            pltpu.VMEM((8, NX) + tile, F32),
            pltpu.VMEM((8, NX) + tile, F32),
            pltpu.VMEM((STEPS, 4) + tile, F32),
            pltpu.VMEM((4, 32, CB), F32),
            pltpu.VMEM((2, TM * STEPS, 32, CB), F32),
            pltpu.VMEM((4, NX) + tile, F32),
            pltpu.VMEM((TM, 4, NX) + tile, F32),
            pltpu.VMEM((TM, 4, NX) + tile, F32),
            pltpu.VMEM((4, NX, 8, NZ), F32),
            dma((2, 4)), dma, dma, dma((TM,)), dma((2, TM)), dma((TM,)),
            dma((4,)), dma((4,)), dma, dma, dma((2,)), dma((2,)), dma((TM,)), dma((TM,)),
            dma((2, TM)), dma((2, TM)), dma((TM,)), dma((TM,)), dma((4,)),
        ],
        compiler_params=pltpu.CompilerParams(
            collective_id=0, has_side_effects=True, vmem_limit_bytes=52 << 20
        ),
        name="sweep",
    )(
        initial_state, heat_source, robin_in, zf,
        source_amplitude, diffusivity, robin_param, spectrum_x,
        spectrum_y[None], spectrum_z[None], open_flag, owner_side,
        xf, yf, yi, xi, zi,
    )


def solution(mesh):
    placed = (
        P("space", "cores", None),
        P("space", "cores", None),
        P("tm"),
        P("space"),
        P("space"),
        P(),
        P("cores"),
        P(),
        P("space", None, "tm", "cores", None),
        P(None, "cores"),
        P(None, "cores"),
    )
    return jax.shard_map(
        local,
        mesh=mesh,
        in_specs=placed,
        out_specs=(P("space", None, "tm", "cores", None), P("tm", "space", "cores", None)),
        check_vma=False,
    )
```

time: 484 us -> 117 us (0.24)
  the two profiles are of different devices: /device:TPU:3 before, /device:TPU:110 now
where the time goes in v1:
time: 117 us; the launch traced here: 115 us
  Pallas kernels  102 us (87%)
  local copies, waits for them, and re-layouts  11.6 us (10%)
  between operations  1.96 us (2%)
    pallas_call x1, Pallas kernels, local(): pl.pallas_call(sweep_kernel, out_shape=(jax.ShapeDtypeStruct((1, 2, STEPS...  102 us
    unnamed x24, local copies, waits for them, and re-layouts  11.6 us

profile of v1, /device:TPU:110, one launch (start us, length us, event | category | flops | bytes accessed | tf_op | source)
XLA Modules:
  0.0 115.2 jit_solution(3021127826427158244)
XLA Ops:
  1.9 0.0 copy-start
  1.9 0.9 copy-done
  2.9 0.0 copy-start.1
  2.9 0.9 copy-done.1
  3.8 0.0 copy-start.2
  3.8 0.9 copy-done.2
  4.8 0.0 copy-start.3
  4.8 0.9 copy-done.3
  5.7 0.0 copy-start.4
  5.7 0.7 copy-done.4
  6.4 0.0 copy-start.5
  6.4 0.7 copy-done.5
  7.2 0.0 copy-start.6
  7.2 0.7 copy-done.6
  7.8 0.0 copy-start.7
  7.8 0.7 copy-done.7
  8.5 0.0 copy-start.8
  8.5 0.7 copy-done.8
  9.2 0.0 copy-start.9
  9.2 0.7 copy-done.9
  9.8 101.6 %sweep.1 = (f32[1,2,8,32,512]{4,3,2,1,0:T(8,128)}, f32[1,32,32,512]{3,2,1,0:T(8,128)}) custom-call(f32[32,32,512]{2,1,0:T(8,128)} %state_in.1, f32[32,32,512]{2,1,0:T(8,128)} %heat_in.1, f32[1,2,8,32,512]{4,3,2,1,0:T(8,128)} %robin_in.1, bf16[4,512,256]{2,1,0:T(8,128)(2,1)} %constant.16.clone.zf_in, f32[8]{0:T(128)S(1)} %copy-done.7, f32[1]{0:T(128)S(6)} %copy.21.diff_s, ...), custom_call_target="tpu_custom_call" | custom-call | tf_op jit(solution)/shard_map/sweep/pallas_call | solution.py:382
  111.4 0.0 copy-start.10
  111.4 2.4 %copy.23 = f32[1,2,8,32,512]{4,3,2,1,0:T(8,128)} copy(f32[1,2,8,32,512]{4,3,2,1,0:T(8,128)} %get-tuple-element.4) | data formatting | bytes 2097152
  113.9 0.0 copy-done.10
  113.9 1.3 %copy.24 = f32[1,32,32,512]{3,2,1,0:T(8,128)} copy(f32[1,32,32,512]{3,2,1,0:T(8,128)S(1)} %copy-done.10) | data formatting | bytes 4194304
Async XLA Ops:
  1.9 1.0 copy-start
  2.9 0.9 copy-start.1
  3.8 0.9 copy-start.2
  4.8 0.9 copy-start.3
  5.7 0.7 copy-start.4
  6.4 0.7 copy-start.5
  7.2 0.7 copy-start.6
  7.8 0.7 copy-start.7
  8.5 0.7 copy-start.8
  9.2 0.7 copy-start.9
  111.4 2.4 %copy-start.10 = (f32[1,32,32,512]{3,2,1,0:T(8,128)S(1)}, f32[1,32,32,512]{3,2,1,0:T(8,128)}, u32[]{:S(2)}) copy-start(f32[1,32,32,512]{3,2,1,0:T(8,128)} %get-tuple-element.5) | copy-start | bytes 6291460

commit v2 on v1

--- a/solution.py
+++ b/solution.py
@@ -65,12 +65,14 @@
 
 def sweep_kernel(
     state_in, heat_in, robin_in, zf_in,
+    amp_in, diff_in, param_in, specx_in, specy_in, specz_in, flag_in, owner_in,
+    xf_in, yf_in, yi_in, xi_in, zi_in,
+    robin_out, ends_out,
     amp_s, diff_s, param_s, specx_s, specy, specz, flag, owner,
     xf, yf, yi, xi, zi,
-    robin_out, ends_out,
-    xin, zf, v, sycol, ptile, amp, rb, modes, src, fac, tr, coef, ob, tbuf, ubuf, wr, acc,
-    s_in, s_zf, s_rl, s_rs, r_rb, s_ro, s_f, r_f, s_y, r_y, s_p, r_p, s_a, r_a,
-    s_o, r_o, s_w, r_w, s_out,
+    xin, zf, v, sycol, ptile, amp, rb, modes, src, fac, tr, coef, ob, st, tbuf, ubuf, wr, acc,
+    s_c, s_in, s_zf, s_rl, s_rs, r_rb, s_ro, s_f, r_f, s_y, r_y, s_p, r_p, s_a, r_a,
+    s_1, r_1, s_1l, s_o, r_o, s_w, r_w, s_out,
 ):
     s = lax.axis_index("space")
     w = lax.axis_index("tm")
@@ -90,6 +92,14 @@
     ins = (state_in, heat_in)
     zf_copy = pltpu.make_async_copy(zf_in.at[w], zf, s_zf)
     zf_copy.start()
+    operands = (
+        (amp_in, amp_s), (param_in, param_s), (specy_in, specy), (xf_in, xf), (diff_in, diff_s),
+        (specx_in, specx_s), (specz_in, specz), (flag_in, flag), (owner_in, owner),
+        (yf_in, yf), (yi_in, yi), (xi_in, xi), (zi_in, zi),
+    )
+    loads = [pltpu.make_async_copy(a, b, s_c.at[i]) for i, (a, b) in enumerate(operands)]
+    for c in loads[:4]:
+        c.start()
 
     def load(i, yt):
         rows = pl.ds(pl.multiple_of(yt * 8, 8), 8)
@@ -104,14 +114,14 @@
 
     own_robin = pltpu.make_async_copy(robin_block(w), rb.at[h, w], s_rl)
     own_robin.start()
+    for c in loads[4:]:
+        c.start()
 
     barrier = pltpu.get_barrier_semaphore()
     for d in range(1, TM):
         pl.semaphore_signal(barrier, inc=1, device_id=(s, other(d), h), device_id_type=MESH)
-    for d in range(TM):
-        pl.semaphore_signal(barrier, inc=1, device_id=(s, other(d), oh), device_id_type=MESH)
-        pl.semaphore_signal(barrier, inc=1, device_id=(left, other(d), h), device_id_type=MESH)
-        pl.semaphore_signal(barrier, inc=1, device_id=(right, other(d), h), device_id_type=MESH)
+    for to in ((s, w, oh), (left, w, h), (right, w, h)):
+        pl.semaphore_signal(barrier, inc=1, device_id=to, device_id_type=MESH)
 
     def column(row):
         n = row.shape[1]
@@ -119,11 +129,13 @@
         picked = jnp.where(on, jnp.broadcast_to(row, (n, n)), 0.0)
         return jnp.broadcast_to(jnp.sum(picked, axis=1, keepdims=True), (n, CB))
 
+    for c in loads[:3]:
+        c.wait()
     for j in range(STEPS):
         amp[w, j] = jnp.full((8, CB), amp_s[j], F32)
     ptile[1] = jnp.full((8, CB), param_s[0], F32)
     sycol[h] = column(specy[...])
-    pl.semaphore_wait(barrier, 15)
+    pl.semaphore_wait(barrier, 6)
 
     small = [
         remote(sycol.at[h], sycol.at[h], s_y, r_y, (s, w, oh)),
@@ -144,6 +156,7 @@
         return remote(v.at[h, yt], v.at[h, yt], s_f.at[yt], r_f.at[yt], (s, w, oh))
 
     zf_copy.wait()
+    loads[3].wait()
 
     def fwd_chunk(yt, carry):
         rows = pl.ds(pl.multiple_of(yt * 8, 8), 8)
@@ -161,9 +174,8 @@
 
     lax.fori_loop(0, 4, fwd_chunk, 0)
 
-    pl_copy = small
-    for c in pl_copy[:3]:
-        c.wait_send()
+    for c in loads[4:9]:
+        c.wait()
     remote(sycol.at[oh], sycol.at[oh], s_y, r_y, (s, w, oh)).wait_recv()
     small[1].wait_recv()
     small[2].wait_recv()
@@ -195,11 +207,19 @@
 
     for yt in range(4):
         fwd_send(yt).wait_send()
-    def cross(d):
-        return remote(robin_block(other(d)), rb.at[h, w], s_ro.at[d], r_rb.at[h, w], (s, other(d), oh))
-
-    for d in range(TM):
-        cross(d).start()
+    own_robin.wait()
+    for d in range(1, TM):
+        f = other(d)
+        remote(rb.at[h, f], rb.at[h, f], s_rs.at[d], r_rb.at[h, f], (s, f, h)).wait_recv()
+        remote(amp.at[f], amp.at[f], s_a.at[d], r_a.at[f], (s, f, h)).wait_recv()
+
+    def cross(k):
+        return remote(rb.at[h, k], rb.at[h, k], s_ro.at[k], r_rb.at[h, k], (s, w, oh))
+
+    for k in range(2):
+        cross(k).start()
+    for c in loads[9:]:
+        c.wait()
 
     for yt in range(4):
         remote(v.at[oh, yt], v.at[oh, yt], s_f.at[yt], r_f.at[yt], (s, w, oh)).wait_recv()
@@ -213,12 +233,6 @@
         return carry
 
     lax.fori_loop(0, 8, y_forward, 0)
-
-    own_robin.wait()
-    for d in range(1, TM):
-        f = other(d)
-        remote(rb.at[h, f], rb.at[h, f], s_rs.at[d], r_rb.at[h, f], (s, f, h)).wait_recv()
-        remote(amp.at[f], amp.at[f], s_a.at[d], r_a.at[f], (s, f, h)).wait_recv()
 
     def steps(k, half, bt, traces):
         tile = half * 4 + bt
@@ -261,18 +275,30 @@
         steps(k, h, bt, True)
         return carry
 
-    def robin_send(side, k):
-        to = left if side == 1 else right
-        return remote(
-            ob.at[side, pl.ds(pl.multiple_of(k * STEPS, STEPS), STEPS)],
-            robin_out.at[0, side, :, :, pl.ds(pl.multiple_of(w * CB, CB), CB)],
-            s_o.at[side, k], r_o.at[side, w], (to, k, h),
-        )
+    lanes = pl.ds(pl.multiple_of(w * CB, CB), CB)
+
+    def block(side, k):
+        return ob.at[side, pl.ds(pl.multiple_of(k * STEPS, STEPS), STEPS)]
+
+    def window_send(side, k):
+        return remote(block(side, k), st.at[side, :, :, lanes], s_1.at[side, k], r_1.at[side, w], (s, k, h))
+
+    def window_keep(side):
+        return pltpu.make_async_copy(block(side, w), st.at[side, :, :, lanes], s_1l.at[side])
 
     def own_window(k, carry):
         lax.fori_loop(k * 4, k * 4 + 4, own_steps, 0)
-        robin_send(0, k).start()
-        robin_send(1, k).start()
+
+        @pl.when(k != w)
+        def _():
+            window_send(0, k).start()
+            window_send(1, k).start()
+
+        @pl.when(k == w)
+        def _():
+            window_keep(0).start()
+            window_keep(1).start()
+
         return carry
 
     lax.fori_loop(0, TM, own_window, 0)
@@ -280,8 +306,33 @@
     def end_send(k):
         return remote(ubuf.at[k], wr.at[w], s_w.at[k], r_w.at[w], (s, k, h))
 
+    def robin_send(side):
+        return remote(
+            st.at[side], robin_out.at[0, side], s_o.at[side], r_o.at[side],
+            (left if side == 1 else right, w, h),
+        )
+
+    def finish_robin():
+        for side in range(2):
+            window_keep(side).wait()
+            for d in range(1, TM):
+                f = other(d)
+                to = st.at[side, :, :, pl.ds(pl.multiple_of(f * CB, CB), CB)]
+                remote(block(side, f), to, s_1.at[side, f], r_1.at[side, f], (s, f, h)).wait_recv()
+            robin_send(side).start()
+
     def other_window(k, carry):
-        remote(rb.at[oh, k], rb.at[oh, k], s_ro.at[0], r_rb.at[oh, k], (s, k, oh)).wait_recv()
+        remote(rb.at[oh, k], rb.at[oh, k], s_ro.at[k], r_rb.at[oh, k], (s, w, oh)).wait_recv()
+        cross(k).wait_send()
+
+        @pl.when(k < TM - 2)
+        def _():
+            cross(k + 2).start()
+
+        @pl.when(k == TM - 1)
+        def _():
+            finish_robin()
+
 
         def body(bt, c):
             steps(k, oh, bt, False)
@@ -347,24 +398,16 @@
     for yt in range(4):
         store(yt).start()
 
-    for c in small[3:]:
+    for c in small:
         c.wait_send()
     for c in same_half:
         c.wait_send()
-    for d in range(TM):
-        cross(d).wait_send()
-    for k in range(TM):
+    for d in range(1, TM):
         for side in range(2):
-            robin_send(side, k).wait_send()
-    for d in range(1, TM):
+            window_send(side, other(d)).wait_send()
         end_send(other(d)).wait_send()
-    for k in range(TM):
-        for side in range(2):
-            remote(
-                ob.at[side, pl.ds(k * STEPS, STEPS)],
-                robin_out.at[0, side, :, :, pl.ds(k * CB, CB)],
-                s_o.at[side, k], r_o.at[side, k], (left, k, h),
-            ).wait_recv()
+    for side in range(2):
+        robin_send(side).wait()
     for yt in range(4):
         store(yt).wait()
 
@@ -374,9 +417,7 @@
     spectrum_x, spectrum_y, spectrum_z, robin_in, open_flag, owner_side,
 ):
     xf, yf, yi, xi, zf, zi = (jnp.asarray(c) for c in constants())
-    any_spec = pl.BlockSpec(memory_space=pl.ANY)
-    smem = pl.BlockSpec(memory_space=pltpu.SMEM)
-    vmem = pl.BlockSpec(memory_space=pltpu.VMEM)
+    hbm = pl.BlockSpec(memory_space=pltpu.HBM)
     dma = pltpu.SemaphoreType.DMA
     tile = (8, CB)
     return pl.pallas_call(
@@ -385,9 +426,15 @@
             jax.ShapeDtypeStruct((1, 2, STEPS, 32, NZ), F32),
             jax.ShapeDtypeStruct((1, NX, 32, NZ), F32),
         ),
-        in_specs=[any_spec] * 4 + [smem] * 4 + [vmem] * 9,
-        out_specs=(any_spec, any_spec),
+        in_specs=[hbm] * 17,
+        out_specs=(hbm, hbm),
         scratch_shapes=[
+            pltpu.SMEM((STEPS,), F32), pltpu.SMEM((1,), F32), pltpu.SMEM((1,), F32),
+            pltpu.SMEM((NX,), F32),
+            pltpu.VMEM((1, 32), F32), pltpu.VMEM((1, NZ), F32),
+            pltpu.VMEM((SPACE, 32), jnp.int32), pltpu.VMEM((SPACE, 32), jnp.int32),
+            pltpu.VMEM(xf.shape, BF16), pltpu.VMEM(yf.shape, BF16), pltpu.VMEM(yi.shape, BF16),
+            pltpu.VMEM(xi.shape, BF16), pltpu.VMEM(zi.shape, BF16),
             pltpu.VMEM((2, NX, 32, NZ), F32),
             pltpu.VMEM((NZ, 2 * CB), BF16),
             pltpu.VMEM((2, 4, 2, NX) + tile, F32),
@@ -401,16 +448,18 @@
             pltpu.VMEM((STEPS, 4) + tile, F32),
             pltpu.VMEM((4, 32, CB), F32),
             pltpu.VMEM((2, TM * STEPS, 32, CB), F32),
+            pltpu.VMEM((2, STEPS, 32, NZ), F32),
             pltpu.VMEM((4, NX) + tile, F32),
             pltpu.VMEM((TM, 4, NX) + tile, F32),
             pltpu.VMEM((TM, 4, NX) + tile, F32),
             pltpu.VMEM((4, NX, 8, NZ), F32),
-            dma((2, 4)), dma, dma, dma((TM,)), dma((2, TM)), dma((TM,)),
+            dma((13,)), dma((2, 4)), dma, dma, dma((TM,)), dma((2, TM)), dma((TM,)),
             dma((4,)), dma((4,)), dma, dma, dma((2,)), dma((2,)), dma((TM,)), dma((TM,)),
-            dma((2, TM)), dma((2, TM)), dma((TM,)), dma((TM,)), dma((4,)),
+            dma((2, TM)), dma((2, TM)), dma((2,)), dma((2,)), dma((2,)),
+            dma((TM,)), dma((TM,)), dma((4,)),
         ],
         compiler_params=pltpu.CompilerParams(
-            collective_id=0, has_side_effects=True, vmem_limit_bytes=52 << 20
+            collective_id=0, has_side_effects=True, vmem_limit_bytes=60 << 20
         ),
         name="sweep",
     )(

time: 117 us -> 91.8 us (0.78); the launches traced: 115 us -> 91.7 us
  Pallas kernels: 102 us -> 86 us
  local copies, waits for them, and re-layouts: 11.6 us -> 3.76 us
    pallas_call x1, Pallas kernels: 102 us -> 86 us  [local(): pl.pallas_call(sweep_kernel, out_shape=(jax.ShapeDtypeStruct((1, 2, STEPS...]
    unnamed x24 -> x4, local copies, waits for them, and re-layouts: 11.6 us -> 3.76 us
where the time goes in v2:
time: 91.8 us; the launch traced here: 91.7 us
  Pallas kernels  86 us (94%)
  local copies, waits for them, and re-layouts  3.76 us (4%)
  between operations  1.94 us (2%)
    pallas_call x1, Pallas kernels, local(): pl.pallas_call(sweep_kernel, out_shape=(jax.ShapeDtypeStruct((1, 2, STEPS...  86 us
    unnamed x4, local copies, waits for them, and re-layouts  3.76 us

profile of v2, /device:TPU:110, one launch (start us, length us, event | category | flops | bytes accessed | tf_op | source)
XLA Modules:
  0.0 91.7 jit_solution(7887243813927873852)
XLA Ops:
  1.9 86.0 %sweep.1 = (f32[1,2,8,32,512]{4,3,2,1,0:T(8,128)}, f32[1,32,32,512]{3,2,1,0:T(8,128)}) custom-call(f32[32,32,512]{2,1,0:T(8,128)} %state_in.1, f32[32,32,512]{2,1,0:T(8,128)} %heat_in.1, f32[1,2,8,32,512]{4,3,2,1,0:T(8,128)} %robin_in.1, bf16[4,512,256]{2,1,0:T(8,128)(2,1)} %constant.16.clone.zf_in, f32[8]{0:T(128)} %amp_in.1, f32[1]{0:T(128)S(6)} %copy.21.diff_in, ...), custom_call_target="tpu_custom_call" | custom-call | tf_op jit(solution)/shard_map/sweep/pallas_call | solution.py:423
  87.9 0.0 copy-start
  87.9 2.4 %copy.23 = f32[1,2,8,32,512]{4,3,2,1,0:T(8,128)} copy(f32[1,2,8,32,512]{4,3,2,1,0:T(8,128)} %get-tuple-element.4) | data formatting | bytes 2097152
  90.3 0.0 copy-done
  90.3 1.3 %copy.24 = f32[1,32,32,512]{3,2,1,0:T(8,128)} copy(f32[1,32,32,512]{3,2,1,0:T(8,128)S(1)} %copy-done) | data formatting | bytes 4194304
Async XLA Ops:
  87.9 2.4 %copy-start = (f32[1,32,32,512]{3,2,1,0:T(8,128)S(1)}, f32[1,32,32,512]{3,2,1,0:T(8,128)}, u32[]{:S(2)}) copy-start(f32[1,32,32,512]{3,2,1,0:T(8,128)} %get-tuple-element.5) | copy-start | bytes 6291460

commit v3 on v2

--- a/solution.py
+++ b/solution.py
@@ -70,9 +70,9 @@
     robin_out, ends_out,
     amp_s, diff_s, param_s, specx_s, specy, specz, flag, owner,
     xf, yf, yi, xi, zi,
-    xin, zf, v, sycol, ptile, amp, rb, modes, src, fac, tr, coef, ob, st, tbuf, ubuf, wr, acc,
+    xin, zf, v, sycol, ptile, amp, rb, modes, src, fac, tr, coef, ob, st, tbuf, ubuf, wr,
     s_c, s_in, s_zf, s_rl, s_rs, r_rb, s_ro, s_f, r_f, s_y, r_y, s_p, r_p, s_a, r_a,
-    s_1, r_1, s_1l, s_o, r_o, s_w, r_w, s_out,
+    s_1, r_1, s_1l, s_o, r_o, s_w, r_w,
 ):
     s = lax.axis_index("space")
     w = lax.axis_index("tm")
@@ -88,6 +88,12 @@
 
     def other(d):
         return lax.rem(w + d, TM)
+
+    barrier = pltpu.get_barrier_semaphore()
+    for d in range(1, TM):
+        pl.semaphore_signal(barrier, inc=1, device_id=(s, other(d), h), device_id_type=MESH)
+    for to in ((s, w, oh), (left, w, h), (right, w, h)):
+        pl.semaphore_signal(barrier, inc=1, device_id=to, device_id_type=MESH)
 
     ins = (state_in, heat_in)
     zf_copy = pltpu.make_async_copy(zf_in.at[w], zf, s_zf)
@@ -117,12 +123,6 @@
     for c in loads[4:]:
         c.start()
 
-    barrier = pltpu.get_barrier_semaphore()
-    for d in range(1, TM):
-        pl.semaphore_signal(barrier, inc=1, device_id=(s, other(d), h), device_id_type=MESH)
-    for to in ((s, w, oh), (left, w, h), (right, w, h)):
-        pl.semaphore_signal(barrier, inc=1, device_id=to, device_id_type=MESH)
-
     def column(row):
         n = row.shape[1]
         on = lax.broadcasted_iota(jnp.int32, (n, n), 0) == lax.broadcasted_iota(jnp.int32, (n, n), 1)
@@ -135,7 +135,27 @@
         amp[w, j] = jnp.full((8, CB), amp_s[j], F32)
     ptile[1] = jnp.full((8, CB), param_s[0], F32)
     sycol[h] = column(specy[...])
+    def fwd_send(yt):
+        return remote(v.at[h, yt], v.at[h, yt], s_f.at[yt], r_f.at[yt], (s, w, oh))
+
+    zf_copy.wait()
+    loads[3].wait()
+
+    def transform(yt):
+        rows = pl.ds(pl.multiple_of(yt * 8, 8), 8)
+        zs = []
+        for i in range(2):
+            load(i, yt).wait()
+            hi, lo = split(xin[i, :, rows, :].reshape(NX * 8, NZ))
+            both = dot(hi, zf[...])
+            zs.append(both[:, :CB] + (both[:, CB:] + dot(lo, zf[:, :CB])))
+        res = const_dot(xf[0], xf[1], jnp.concatenate(zs, axis=1))
+        v[h, yt, 0] = res[:, :CB].reshape(NX, 8, CB)
+        v[h, yt, 1] = res[:, CB:].reshape(NX, 8, CB)
+
+    transform(0)
     pl.semaphore_wait(barrier, 6)
+    fwd_send(0).start()
 
     small = [
         remote(sycol.at[h], sycol.at[h], s_y, r_y, (s, w, oh)),
@@ -152,27 +172,12 @@
         c.start()
         same_half.append(c)
 
-    def fwd_send(yt):
-        return remote(v.at[h, yt], v.at[h, yt], s_f.at[yt], r_f.at[yt], (s, w, oh))
-
-    zf_copy.wait()
-    loads[3].wait()
-
     def fwd_chunk(yt, carry):
-        rows = pl.ds(pl.multiple_of(yt * 8, 8), 8)
-        zs = []
-        for i in range(2):
-            load(i, yt).wait()
-            hi, lo = split(xin[i, :, rows, :].reshape(NX * 8, NZ))
-            both = dot(hi, zf[...])
-            zs.append(both[:, :CB] + (both[:, CB:] + dot(lo, zf[:, :CB])))
-        res = const_dot(xf[0], xf[1], jnp.concatenate(zs, axis=1))
-        v[h, yt, 0] = res[:, :CB].reshape(NX, 8, CB)
-        v[h, yt, 1] = res[:, CB:].reshape(NX, 8, CB)
+        transform(yt)
         fwd_send(yt).start()
         return carry
 
-    lax.fori_loop(0, 4, fwd_chunk, 0)
+    lax.fori_loop(1, 4, fwd_chunk, 0)
 
     for c in loads[4:9]:
         c.wait()
@@ -374,13 +379,14 @@
 
     def z_inverse(ref, index, b, first):
         def body(yt, c):
+            rows = pl.ds(pl.multiple_of(yt * 8, 8), 8)
             hi, lo = split(ref[index, yt].reshape(NX * 8, CB))
             m_hi, m_lo = zi[0, b], zi[1, b]
             part = (dot(hi, m_hi) + (dot(lo, m_hi) + dot(hi, m_lo))).reshape(NX, 8, NZ)
             if first:
-                acc[yt] = part
+                ends_out[0, :, rows, :] = part
             else:
-                acc[yt] += part
+                ends_out[0, :, rows, :] += part
             return c
 
         lax.fori_loop(0, 4, body, 0)
@@ -390,13 +396,6 @@
         f = other(d)
         remote(ubuf.at[f], wr.at[f], s_w.at[f], r_w.at[f], (s, f, h)).wait_recv()
         z_inverse(wr, f, f, False)
-
-    def store(yt):
-        rows = pl.ds(pl.multiple_of(yt * 8, 8), 8)
-        return pltpu.make_async_copy(acc.at[yt], ends_out.at[0, :, rows, :], s_out.at[yt])
-
-    for yt in range(4):
-        store(yt).start()
 
     for c in small:
         c.wait_send()
@@ -408,8 +407,6 @@
         end_send(other(d)).wait_send()
     for side in range(2):
         robin_send(side).wait()
-    for yt in range(4):
-        store(yt).wait()
 
 
 def local(
@@ -423,11 +420,11 @@
     return pl.pallas_call(
         sweep_kernel,
         out_shape=(
-            jax.ShapeDtypeStruct((1, 2, STEPS, 32, NZ), F32),
-            jax.ShapeDtypeStruct((1, NX, 32, NZ), F32),
+            pltpu.VMEM((1, 2, STEPS, 32, NZ), F32),
+            pltpu.VMEM((1, NX, 32, NZ), F32),
         ),
         in_specs=[hbm] * 17,
-        out_specs=(hbm, hbm),
+        out_specs=(pl.BlockSpec(memory_space=pltpu.VMEM),) * 2,
         scratch_shapes=[
             pltpu.SMEM((STEPS,), F32), pltpu.SMEM((1,), F32), pltpu.SMEM((1,), F32),
             pltpu.SMEM((NX,), F32),
@@ -452,22 +449,21 @@
             pltpu.VMEM((4, NX) + tile, F32),
             pltpu.VMEM((TM, 4, NX) + tile, F32),
             pltpu.VMEM((TM, 4, NX) + tile, F32),
-            pltpu.VMEM((4, NX, 8, NZ), F32),
             dma((13,)), dma((2, 4)), dma, dma, dma((TM,)), dma((2, TM)), dma((TM,)),
             dma((4,)), dma((4,)), dma, dma, dma((2,)), dma((2,)), dma((TM,)), dma((TM,)),
             dma((2, TM)), dma((2, TM)), dma((2,)), dma((2,)), dma((2,)),
-            dma((TM,)), dma((TM,)), dma((4,)),
+            dma((TM,)), dma((TM,)),
         ],
         compiler_params=pltpu.CompilerParams(
-            collective_id=0, has_side_effects=True, vmem_limit_bytes=60 << 20
+            collective_id=0, has_side_effects=True, vmem_limit_bytes=44 << 20
         ),
         name="sweep",
-    )(
+    )(*(v if v.size == 1 else pltpu.with_memory_space_constraint(v, pltpu.HBM) for v in (
         initial_state, heat_source, robin_in, zf,
         source_amplitude, diffusivity, robin_param, spectrum_x,
         spectrum_y[None], spectrum_z[None], open_flag, owner_side,
         xf, yf, yi, xi, zi,
-    )
+    )))
 
 
 def solution(mesh):

time: 91.8 us -> 87 us (0.948)
  Pallas kernels: 86 us -> 81.9 us
  local copies, waits for them, and re-layouts: 3.76 us -> 2.29 us
    pallas_call x1, Pallas kernels: 86 us -> 81.9 us  [local(): pl.pallas_call(sweep_kernel, out_shape=(pltpu.VMEM((1, 2, STEPS, 32, NZ),...]
    unnamed x4 -> x2, local copies, waits for them, and re-layouts: 3.76 us -> 2.29 us
where the time goes in v3:
time: 87 us; the launch traced here: 86.1 us
  Pallas kernels  81.9 us (94%)
  local copies, waits for them, and re-layouts  2.29 us (3%)
  between operations  1.93 us (2%)
    pallas_call x1, Pallas kernels, local(): pl.pallas_call(sweep_kernel, out_shape=(pltpu.VMEM((1, 2, STEPS, 32, NZ),...  81.9 us
    unnamed x2, local copies, waits for them, and re-layouts  2.29 us

profile of v3, /device:TPU:110, one launch (start us, length us, event | category | flops | bytes accessed | tf_op | source)
XLA Modules:
  0.0 86.1 jit_solution(12672424692028722701)
XLA Ops:
  1.9 81.9 %sweep.1 = (f32[1,2,8,32,512]{4,3,2,1,0:T(8,128)S(1)}, f32[1,32,32,512]{3,2,1,0:T(8,128)S(1)}) custom-call(f32[32,32,512]{2,1,0:T(8,128)} %state_in.1, f32[32,32,512]{2,1,0:T(8,128)} %heat_in.1, f32[1,2,8,32,512]{4,3,2,1,0:T(8,128)} %robin_in.1, bf16[4,512,256]{2,1,0:T(8,128)(2,1)} %constant.16.clone.zf_in, f32[8]{0:T(128)} %amp_in.1, f32[1]{0:T(128)S(6)} %copy.23.diff_in, ...), custom_call_target="tpu_custom_call" | custom-call | tf_op jit(solution)/shard_map/sweep/pallas_call | solution.py:420
  83.8 1.0 %copy.21 = f32[1,2,8,32,512]{4,3,2,1,0:T(8,128)} copy(f32[1,2,8,32,512]{4,3,2,1,0:T(8,128)S(1)} %get-tuple-element.2) | data formatting | bytes 2097152
  84.8 1.3 %copy.22 = f32[1,32,32,512]{3,2,1,0:T(8,128)} copy(f32[1,32,32,512]{3,2,1,0:T(8,128)S(1)} %get-tuple-element.3) | data formatting | bytes 4194304

commit v4 on v3

--- a/solution.py
+++ b/solution.py
@@ -13,6 +13,7 @@
 F32, BF16 = jnp.float32, jnp.bfloat16
 NX, NY, NZ, STEPS, TM, SPACE = 32, 64, 512, 8, 4, 32
 CB = NZ // TM
+LANES = CB // 4
 PERM = list(range(0, NX, 2)) + list(range(1, NX, 2))
 
 
@@ -45,7 +46,7 @@
     y_inv = np.stack([split_constant(y_inv[0]), split_constant(y_inv[1])])
     z_fwd = split_constant(C_Z.T)
     z_fwd = z_fwd.reshape(2, NZ, TM, CB).transpose(2, 1, 0, 3).reshape(TM, NZ, 2 * CB)
-    z_inv = split_constant(C_Z).reshape(2, TM, CB, NZ)
+    z_inv = split_constant(C_Z).reshape(2, TM, 4, LANES, NZ).transpose(0, 2, 1, 3, 4).reshape(2, 4, CB, NZ)
     return (split_constant(x_fwd), split_constant(y_fwd), y_inv, split_constant(x_inv), z_fwd, z_inv)
 
 
@@ -61,6 +62,22 @@
 def const_dot(m_hi, m_lo, v):
     hi, lo = split(v)
     return dot(m_hi, hi) + (dot(m_lo, hi) + dot(m_hi, lo))
+
+
+def regroup(tiles):
+    shape = tiles[0].shape
+    t = [x.reshape(-1, CB) for x in tiles]
+    lane = lax.broadcasted_iota(jnp.int32, t[0].shape, 1)
+    low, even = lane < 64, lax.rem(lane, 64) < 32
+    u = [None] * 4
+    for a in (0, 1):
+        u[a] = jnp.where(low, t[a], pltpu.roll(t[a + 2], 64, 1))
+        u[a + 2] = jnp.where(low, pltpu.roll(t[a], 64, 1), t[a + 2])
+    v = [None] * 4
+    for a in (0, 2):
+        v[a] = jnp.where(even, u[a], pltpu.roll(u[a + 1], 32, 1))
+        v[a + 1] = jnp.where(even, pltpu.roll(u[a], 96, 1), u[a + 1])
+    return [x.reshape(shape) for x in v]
 
 
 def sweep_kernel(
@@ -70,9 +87,10 @@
     robin_out, ends_out,
     amp_s, diff_s, param_s, specx_s, specy, specz, flag, owner,
     xf, yf, yi, xi, zi,
-    xin, zf, v, sycol, ptile, amp, rb, modes, src, fac, tr, coef, ob, st, tbuf, ubuf, wr,
-    s_c, s_in, s_zf, s_rl, s_rs, r_rb, s_ro, s_f, r_f, s_y, r_y, s_p, r_p, s_a, r_a,
-    s_1, r_1, s_1l, s_o, r_o, s_w, r_w,
+    xin, zf, v, sycol, ptile, amp, rin, rp, rb, modes, src, fac, tr, coef, ob, ob2, st,
+    tbuf, xbuf, ubuf, wr,
+    s_c, s_in, s_zf, s_rl, s_rs, r_rb, s_ro, r_ro, s_f, r_f, s_y, r_y, s_p, r_p, s_a, r_a,
+    s_1, r_1, s_1l, s_o, r_o, s_w, r_w, s_wl,
 ):
     s = lax.axis_index("space")
     w = lax.axis_index("tm")
@@ -115,10 +133,7 @@
         for i in range(2):
             load(i, yt).start()
 
-    def robin_block(d):
-        return robin_in.at[0, :, :, :, pl.ds(pl.multiple_of(d * CB, CB), CB)]
-
-    own_robin = pltpu.make_async_copy(robin_block(w), rb.at[h, w], s_rl)
+    own_robin = pltpu.make_async_copy(robin_in.at[0], rin, s_rl.at[0])
     own_robin.start()
     for c in loads[4:]:
         c.start()
@@ -166,11 +181,24 @@
         small.append(remote(amp.at[w], amp.at[w], s_a.at[d], r_a.at[w], (s, other(d), h)))
     for c in small:
         c.start()
+    own_robin.wait()
+
+    def pack_robin(p, carry):
+        lanes = pl.ds(pl.multiple_of(p * CB, CB), CB)
+        for side in range(2):
+            got = regroup([rin[side, :, pl.ds(8 * q, 8), lanes] for q in range(4)])
+            for j in range(4):
+                rp[p, j, side] = got[j]
+        return carry
+
+    lax.fori_loop(0, TM, pack_robin, 0)
     same_half = []
     for d in range(1, TM):
-        c = remote(robin_block(other(d)), rb.at[h, w], s_rs.at[d], r_rb.at[h, w], (s, other(d), h))
+        c = remote(rp.at[other(d)], rb.at[h, :, w], s_rs.at[d], r_rb.at[w], (s, other(d), h))
         c.start()
         same_half.append(c)
+    keep_robin = pltpu.make_async_copy(rp.at[w], rb.at[h, :, w], s_rl.at[1])
+    keep_robin.start()
 
     def fwd_chunk(yt, carry):
         transform(yt)
@@ -194,35 +222,43 @@
     pt = [jnp.broadcast_to(ptile[i][0:1], (32, CB)) for i in range(3)]
     o_l, op_l = coefficient(left, pt[0], pt[1])
     o_r, op_r = coefficient(s, pt[1], pt[2])
-    coef[0] = o_l
-    coef[1] = op_l
-    coef[2] = o_r
-    coef[3] = op_r
+    for i, c in enumerate((o_l, op_l, o_r, op_r)):
+        coef[i] = regroup([c[8 * q:8 * q + 8] for q in range(4)])[0]
 
     sz = jnp.broadcast_to(specz[:, pl.ds(pl.multiple_of(w * CB, CB), CB)], (8, CB))
 
-    def factor(bt, carry):
-        sy = sycol[lax.div(bt, 4), pl.ds(pl.multiple_of(lax.rem(bt, 4) * 8, 8), 8), :]
-        for a in range(NX):
-            rate = (specx_s[PERM[a]] + sy) + sz
-            fac[bt, a] = 1.0 / (1.0 + diff_s[0] * rate)
+    sz4 = regroup([sz] * 4)
+    for half in range(2):
+        sy = regroup([sycol[half, pl.ds(8 * q, 8), :] for q in range(4)])[0]
+
+        def factor(a, carry):
+            base = specx_s[a] + sy
+            at = lax.div(a, 2) + lax.rem(a, 2) * (NX // 2)
+            for j in range(4):
+                fac[j, half, at] = 1.0 / (1.0 + diff_s[0] * (base + sz4[j]))
+            return carry
+
+        lax.fori_loop(0, NX, factor, 0)
+
+    def clear(x, carry):
+        ends_out[0, x] = jnp.zeros((32, NZ), F32)
         return carry
 
-    lax.fori_loop(0, 8, factor, 0)
+    lax.fori_loop(0, NX, clear, 0)
 
     for yt in range(4):
         fwd_send(yt).wait_send()
-    own_robin.wait()
+    keep_robin.wait()
     for d in range(1, TM):
         f = other(d)
-        remote(rb.at[h, f], rb.at[h, f], s_rs.at[d], r_rb.at[h, f], (s, f, h)).wait_recv()
+        remote(rb.at[h, :, f], rb.at[h, :, f], s_rs.at[d], r_rb.at[f], (s, f, h)).wait_recv()
         remote(amp.at[f], amp.at[f], s_a.at[d], r_a.at[f], (s, f, h)).wait_recv()
 
-    def cross(k):
-        return remote(rb.at[h, k], rb.at[h, k], s_ro.at[k], r_rb.at[h, k], (s, w, oh))
-
-    for k in range(2):
-        cross(k).start()
+    def cross(j):
+        return remote(rb.at[h, j], rb.at[h, j], s_ro.at[j], r_ro.at[j], (s, w, oh))
+
+    for j in range(2):
+        cross(j).start()
     for c in loads[9:]:
         c.wait()
 
@@ -233,25 +269,30 @@
         at = pl.ds(g * 4, 4)
         rhs = jnp.concatenate([v[:, :, i, at].reshape(256, CB) for i in range(2)], axis=1)
         res = const_dot(yf[0], yf[1], rhs)
-        modes[0, :, at] = res[:, :CB].reshape(8, 4, 8, CB)
-        src[:, at] = res[:, CB:].reshape(8, 4, 8, CB)
+        both = res.reshape(8, 4, 8, 2 * CB)
+        for half in range(2):
+            tiles = both[4 * half:4 * half + 4]
+            got = regroup([tiles[q][:, :, :CB] for q in range(4)])
+            for j in range(4):
+                modes[0, j, half, at] = got[j]
+            got = regroup([tiles[q][:, :, CB:] for q in range(4)])
+            for j in range(4):
+                src[j, half, at] = got[j]
         return carry
 
     lax.fori_loop(0, 8, y_forward, 0)
 
-    def steps(k, half, bt, traces):
-        tile = half * 4 + bt
-        rows = pl.ds(pl.multiple_of(bt * 8, 8), 8)
+    def steps(k, half, j, traces):
         for g in range(4):
             a0 = g * 8
-            mu = [modes[k, tile, a0 + i] for i in range(8)]
-            fs = [fac[tile, a0 + i] for i in range(8)]
-            sg = [src[tile, a0 + i] for i in range(8)]
-            for j in range(STEPS):
-                r0 = rb[half, k, 0, j, rows, :]
-                r1 = rb[half, k, 1, j, rows, :]
+            mu = [modes[k, j, half, a0 + i] for i in range(8)]
+            fs = [fac[j, half, a0 + i] for i in range(8)]
+            sg = [src[j, half, a0 + i] for i in range(8)]
+            for t in range(STEPS):
+                r0 = rb[half, j, k, 0, t]
+                r1 = rb[half, j, k, 1, t]
                 p = r0 + r1 if g < 2 else r0 - r1
-                am = amp[k, j]
+                am = amp[k, t]
                 for i in range(8):
                     mu[i] = (mu[i] + (am * sg[i] + p)) * fs[i]
                 if traces:
@@ -260,30 +301,24 @@
                     val = sum(val[1:], val[0])
                     slo = sum(slo[1:], slo[0])
                     if g % 2 == 0:
-                        tr[j, g] = val
-                        tr[j, g + 1] = slo
+                        tr[t, g] = val
+                        tr[t, g + 1] = slo
                     elif g == 1:
-                        tr[j, 0] += val
-                        tr[j, 1] += slo
+                        tr[t, 0] += val
+                        tr[t, 1] += slo
                     else:
-                        e0, e1 = tr[j, 0], tr[j, 1]
-                        o0 = tr[j, 2] + val
-                        o1 = tr[j, 3] + slo
-                        at = k * STEPS + j
-                        ob[1, at, rows, :] = coef[0, rows, :] * (e1 + o1) + coef[1, rows, :] * (e0 + o0)
-                        ob[0, at, rows, :] = coef[3, rows, :] * (e0 - o0) - coef[2, rows, :] * (o1 - e1)
+                        e0, e1 = tr[t, 0], tr[t, 1]
+                        o0 = tr[t, 2] + val
+                        o1 = tr[t, 3] + slo
+                        ob[1, j, t] = coef[0] * (e1 + o1) + coef[1] * (e0 + o0)
+                        ob[0, j, t] = coef[3] * (e0 - o0) - coef[2] * (o1 - e1)
             for i in range(8):
-                modes[k + 1, tile, a0 + i] = mu[i]
-
-    def own_steps(t, carry):
-        k, bt = lax.div(t, 4), lax.rem(t, 4)
-        steps(k, h, bt, True)
-        return carry
+                modes[k + 1, j, half, a0 + i] = mu[i]
 
     lanes = pl.ds(pl.multiple_of(w * CB, CB), CB)
 
     def block(side, k):
-        return ob.at[side, pl.ds(pl.multiple_of(k * STEPS, STEPS), STEPS)]
+        return ob2.at[side, k]
 
     def window_send(side, k):
         return remote(block(side, k), st.at[side, :, :, lanes], s_1.at[side, k], r_1.at[side, w], (s, k, h))
@@ -292,7 +327,15 @@
         return pltpu.make_async_copy(block(side, w), st.at[side, :, :, lanes], s_1l.at[side])
 
     def own_window(k, carry):
-        lax.fori_loop(k * 4, k * 4 + 4, own_steps, 0)
+        def own_steps(j, c):
+            steps(k, h, j, True)
+            return c
+
+        lax.fori_loop(0, 4, own_steps, 0)
+        for side in range(2):
+            got = regroup([ob[side, j] for j in range(4)])
+            for q in range(4):
+                ob2[side, k, :, pl.ds(8 * q, 8), :] = got[q]
 
         @pl.when(k != w)
         def _():
@@ -308,8 +351,11 @@
 
     lax.fori_loop(0, TM, own_window, 0)
 
-    def end_send(k):
-        return remote(ubuf.at[k], wr.at[w], s_w.at[k], r_w.at[w], (s, k, h))
+    def end_send(j, k):
+        return remote(ubuf.at[j, k], wr.at[j, w], s_w.at[j, k], r_w.at[j, w], (s, k, h))
+
+    def end_keep(j):
+        return pltpu.make_async_copy(ubuf.at[j, w], wr.at[j, w], s_wl.at[j])
 
     def robin_send(side):
         return remote(
@@ -326,34 +372,40 @@
                 remote(block(side, f), to, s_1.at[side, f], r_1.at[side, f], (s, f, h)).wait_recv()
             robin_send(side).start()
 
-    def other_window(k, carry):
-        remote(rb.at[oh, k], rb.at[oh, k], s_ro.at[k], r_rb.at[oh, k], (s, w, oh)).wait_recv()
-        cross(k).wait_send()
-
-        @pl.when(k < TM - 2)
+    def quarter(j, carry):
+        remote(rb.at[oh, j], rb.at[oh, j], s_ro.at[j], r_ro.at[j], (s, w, oh)).wait_recv()
+        cross(j).wait_send()
+
+        @pl.when(j < 2)
         def _():
-            cross(k + 2).start()
-
-        @pl.when(k == TM - 1)
+            cross(j + 2).start()
+
+        @pl.when(j == 3)
         def _():
             finish_robin()
 
-
-        def body(bt, c):
-            steps(k, oh, bt, False)
+        def body(k, c):
+            steps(k, oh, j, False)
             return c
 
-        lax.fori_loop(0, 4, body, 0)
+        lax.fori_loop(0, TM, body, 0)
         my_hi, my_lo = yi[h, 0], yi[h, 1]
 
         def y_inverse(g, c):
-            a, b = pl.ds(g * 8, 4), pl.ds(g * 8 + 4, 4)
+            at = pl.ds(pl.multiple_of(g * 8, 8), 8)
+            tiles = []
+            for half in range(2):
+                tiles += regroup([modes[k + 1, j, half, at] for k in range(TM)])
             rhs = jnp.concatenate(
-                [modes[k + 1, :, a].reshape(256, CB), modes[k + 1, :, b].reshape(256, CB)], axis=1
+                [
+                    jnp.concatenate([x[4 * i:4 * i + 4].reshape(32, CB) for x in tiles], axis=0)
+                    for i in range(2)
+                ],
+                axis=1,
             )
             res = const_dot(my_hi, my_lo, rhs)
-            tbuf[:, a] = res[:, :CB].reshape(4, 4, 8, CB)
-            tbuf[:, b] = res[:, CB:].reshape(4, 4, 8, CB)
+            tbuf[:, pl.ds(g * 8, 4)] = res[:, :CB].reshape(4, 4, 8, CB)
+            tbuf[:, pl.ds(g * 8 + 4, 4)] = res[:, CB:].reshape(4, 4, 8, CB)
             return c
 
         lax.fori_loop(0, 4, y_inverse, 0)
@@ -363,39 +415,50 @@
                 [tbuf[2 * q].reshape(256, CB), tbuf[2 * q + 1].reshape(256, CB)], axis=1
             )
             res = const_dot(xi[0], xi[1], rhs)
-            ubuf[k, 2 * q] = res[:, :CB].reshape(NX, 8, CB)
-            ubuf[k, 2 * q + 1] = res[:, CB:].reshape(NX, 8, CB)
+            xbuf[2 * q] = res[:, :CB].reshape(NX, 8, CB)
+            xbuf[2 * q + 1] = res[:, CB:].reshape(NX, 8, CB)
             return c
 
         lax.fori_loop(0, 2, x_inverse, 0)
 
-        @pl.when(k != w)
+        def by_window(i, c):
+            at = pl.ds(pl.multiple_of(i * 8, 8), 8)
+            got = regroup([xbuf[yt, at] for yt in range(4)])
+            for k in range(TM):
+                ubuf[j, k, at] = got[k]
+            return c
+
+        lax.fori_loop(0, 4, by_window, 0)
+        for d in range(1, TM):
+            end_send(j, other(d)).start()
+        end_keep(j).start()
+
+        @pl.when(j > 0)
         def _():
-            end_send(k).start()
+            z_inverse(j - 1)
 
         return carry
 
-    lax.fori_loop(0, TM, other_window, 0)
-
-    def z_inverse(ref, index, b, first):
-        def body(yt, c):
-            rows = pl.ds(pl.multiple_of(yt * 8, 8), 8)
-            hi, lo = split(ref[index, yt].reshape(NX * 8, CB))
-            m_hi, m_lo = zi[0, b], zi[1, b]
-            part = (dot(hi, m_hi) + (dot(lo, m_hi) + dot(hi, m_lo))).reshape(NX, 8, NZ)
-            if first:
-                ends_out[0, :, rows, :] = part
-            else:
-                ends_out[0, :, rows, :] += part
+    def z_inverse(j):
+        end_keep(j).wait()
+        for d in range(1, TM):
+            f = other(d)
+            remote(ubuf.at[j, f], wr.at[j, f], s_w.at[j, f], r_w.at[j, f], (s, f, h)).wait_recv()
+
+        def body(i, c):
+            at = pl.ds(pl.multiple_of(i * 8, 8), 8)
+            got = regroup([wr[j, p, at] for p in range(TM)])
+            hi, lo = split(jnp.concatenate([x.reshape(64, CB) for x in got], axis=0))
+            m_hi, m_lo = zi[0, j], zi[1, j]
+            part = dot(hi, m_hi) + (dot(lo, m_hi) + dot(hi, m_lo))
+            for yt in range(4):
+                ends_out[0, at, pl.ds(8 * yt, 8), :] += part[64 * yt:64 * yt + 64].reshape(8, 8, NZ)
             return c
 
         lax.fori_loop(0, 4, body, 0)
 
-    z_inverse(ubuf, w, w, True)
-    for d in (1, 3, 2):
-        f = other(d)
-        remote(ubuf.at[f], wr.at[f], s_w.at[f], r_w.at[f], (s, f, h)).wait_recv()
-        z_inverse(wr, f, f, False)
+    lax.fori_loop(0, 4, quarter, 0)
+    z_inverse(3)
 
     for c in small:
         c.wait_send()
@@ -404,7 +467,8 @@
     for d in range(1, TM):
         for side in range(2):
             window_send(side, other(d)).wait_send()
-        end_send(other(d)).wait_send()
+        for j in range(4):
+            end_send(j, other(d)).wait_send()
     for side in range(2):
         robin_send(side).wait()
 
@@ -438,21 +502,25 @@
             pltpu.VMEM((2, 32, CB), F32),
             pltpu.VMEM((3,) + tile, F32),
             pltpu.VMEM((TM, STEPS) + tile, F32),
-            pltpu.VMEM((2, TM, 2, STEPS, 32, CB), F32),
-            pltpu.VMEM((TM + 1, 8, NX) + tile, F32),
-            pltpu.VMEM((8, NX) + tile, F32),
-            pltpu.VMEM((8, NX) + tile, F32),
+            pltpu.VMEM((2, STEPS, 32, NZ), F32),
+            pltpu.VMEM((TM, 4, 2, STEPS) + tile, F32),
+            pltpu.VMEM((2, 4, TM, 2, STEPS) + tile, F32),
+            pltpu.VMEM((TM + 1, 4, 2, NX) + tile, F32),
+            pltpu.VMEM((4, 2, NX) + tile, F32),
+            pltpu.VMEM((4, 2, NX) + tile, F32),
             pltpu.VMEM((STEPS, 4) + tile, F32),
-            pltpu.VMEM((4, 32, CB), F32),
-            pltpu.VMEM((2, TM * STEPS, 32, CB), F32),
+            pltpu.VMEM((4,) + tile, F32),
+            pltpu.VMEM((2, 4, STEPS) + tile, F32),
+            pltpu.VMEM((2, TM, STEPS, 32, CB), F32),
             pltpu.VMEM((2, STEPS, 32, NZ), F32),
             pltpu.VMEM((4, NX) + tile, F32),
-            pltpu.VMEM((TM, 4, NX) + tile, F32),
-            pltpu.VMEM((TM, 4, NX) + tile, F32),
-            dma((13,)), dma((2, 4)), dma, dma, dma((TM,)), dma((2, TM)), dma((TM,)),
+            pltpu.VMEM((4, NX) + tile, F32),
+            pltpu.VMEM((4, TM, NX) + tile, F32),
+            pltpu.VMEM((4, TM, NX) + tile, F32),
+            dma((13,)), dma((2, 4)), dma, dma((2,)), dma((TM,)), dma((TM,)), dma((4,)), dma((4,)),
             dma((4,)), dma((4,)), dma, dma, dma((2,)), dma((2,)), dma((TM,)), dma((TM,)),
             dma((2, TM)), dma((2, TM)), dma((2,)), dma((2,)), dma((2,)),
-            dma((TM,)), dma((TM,)),
+            dma((4, TM)), dma((4, TM)), dma((4,)),
         ],
         compiler_params=pltpu.CompilerParams(
             collective_id=0, has_side_effects=True, vmem_limit_bytes=44 << 20

time: 87 us -> 88.1 us (1.013)
  the two profiles are of different devices: /device:TPU:110 before, /device:TPU:7 now
where the time goes in v4:
time: 88.1 us; the launch traced here: 88 us
  Pallas kernels  83.8 us (95%)
  local copies, waits for them, and re-layouts  2.29 us (3%)
  between operations  1.93 us (2%)
    pallas_call x1, Pallas kernels, local(): pl.pallas_call(sweep_kernel, out_shape=(pltpu.VMEM((1, 2, STEPS, 32, NZ),...  83.8 us
    unnamed x2, local copies, waits for them, and re-layouts  2.29 us

profile of v4, /device:TPU:7, one launch (start us, length us, event | category | flops | bytes accessed | tf_op | source)
XLA Modules:
  0.0 88.0 jit_solution(2627513940491165581)
XLA Ops:
  1.9 83.8 %sweep.1 = (f32[1,2,8,32,512]{4,3,2,1,0:T(8,128)S(1)}, f32[1,32,32,512]{3,2,1,0:T(8,128)S(1)}) custom-call(f32[32,32,512]{2,1,0:T(8,128)} %state_in.1, f32[32,32,512]{2,1,0:T(8,128)} %heat_in.1, f32[1,2,8,32,512]{4,3,2,1,0:T(8,128)} %robin_in.1, bf16[4,512,256]{2,1,0:T(8,128)(2,1)} %constant.16.clone.zf_in, f32[8]{0:T(128)} %amp_in.1, f32[1]{0:T(128)S(6)} %copy.23.diff_in, ...), custom_call_target="tpu_custom_call" | custom-call | tf_op jit(solution)/shard_map/sweep/pallas_call | solution.py:484
  85.7 1.0 %copy.21 = f32[1,2,8,32,512]{4,3,2,1,0:T(8,128)} copy(f32[1,2,8,32,512]{4,3,2,1,0:T(8,128)S(1)} %get-tuple-element.2) | data formatting | bytes 2097152
  86.7 1.3 %copy.22 = f32[1,32,32,512]{3,2,1,0:T(8,128)} copy(f32[1,32,32,512]{3,2,1,0:T(8,128)S(1)} %get-tuple-element.3) | data formatting | bytes 4194304

commit v5 on v4

--- a/solution.py
+++ b/solution.py
@@ -47,6 +47,7 @@
     z_fwd = split_constant(C_Z.T)
     z_fwd = z_fwd.reshape(2, NZ, TM, CB).transpose(2, 1, 0, 3).reshape(TM, NZ, 2 * CB)
     z_inv = split_constant(C_Z).reshape(2, TM, 4, LANES, NZ).transpose(0, 2, 1, 3, 4).reshape(2, 4, CB, NZ)
+    z_inv = np.concatenate([z_inv[0], z_inv[0], z_inv[1]], axis=1)
     return (split_constant(x_fwd), split_constant(y_fwd), y_inv, split_constant(x_inv), z_fwd, z_inv)
 
 
@@ -87,9 +88,9 @@
     robin_out, ends_out,
     amp_s, diff_s, param_s, specx_s, specy, specz, flag, owner,
     xf, yf, yi, xi, zi,
-    xin, zf, v, sycol, ptile, amp, rin, rp, rb, modes, src, fac, tr, coef, ob, ob2, st,
+    xin, zf, vt, v, sycol, ptile, amp, rin, rp, rb, modes, src, fac, tr, coef, ob, st1, st,
     tbuf, xbuf, ubuf, wr,
-    s_c, s_in, s_zf, s_rl, s_rs, r_rb, s_ro, r_ro, s_f, r_f, s_y, r_y, s_p, r_p, s_a, r_a,
+    s_c, s_in, s_zf, s_rl, s_rs, r_rb, s_cw, r_cw, s_ro, r_ro, s_f, r_f, s_y, r_y, s_p, r_p, s_a, r_a,
     s_1, r_1, s_1l, s_o, r_o, s_w, r_w, s_wl,
 ):
     s = lax.axis_index("space")
@@ -114,6 +115,8 @@
         pl.semaphore_signal(barrier, inc=1, device_id=to, device_id_type=MESH)
 
     ins = (state_in, heat_in)
+    own_robin = pltpu.make_async_copy(robin_in.at[0], rin, s_rl.at[0])
+    own_robin.start()
     zf_copy = pltpu.make_async_copy(zf_in.at[w], zf, s_zf)
     zf_copy.start()
     operands = (
@@ -133,8 +136,6 @@
         for i in range(2):
             load(i, yt).start()
 
-    own_robin = pltpu.make_async_copy(robin_in.at[0], rin, s_rl.at[0])
-    own_robin.start()
     for c in loads[4:]:
         c.start()
 
@@ -150,13 +151,36 @@
         amp[w, j] = jnp.full((8, CB), amp_s[j], F32)
     ptile[1] = jnp.full((8, CB), param_s[0], F32)
     sycol[h] = column(specy[...])
-    def fwd_send(yt):
-        return remote(v.at[h, yt], v.at[h, yt], s_f.at[yt], r_f.at[yt], (s, w, oh))
+    own_robin.wait()
+
+    def pack_robin(p, carry):
+        lanes = pl.ds(pl.multiple_of(p * CB, CB), CB)
+        for side in range(2):
+            got = regroup([rin[side, :, pl.ds(8 * q, 8), lanes] for q in range(4)])
+            for j in range(4):
+                rp[p, j, side] = got[j]
+        return carry
+
+    pack_robin(w, 0)
+    pl.semaphore_wait(barrier, 6)
+    cross_own = remote(rp.at[w], rb.at[h, :, w], s_cw, r_cw, (s, w, oh))
+    cross_own.start()
+    keep_robin = pltpu.make_async_copy(rp.at[w], rb.at[h, :, w], s_rl.at[1])
+    keep_robin.start()
+    same_half = []
+    for d in range(1, TM):
+        pack_robin(other(d), 0)
+        c = remote(rp.at[other(d)], rb.at[h, :, w], s_rs.at[d], r_rb.at[w], (s, other(d), h))
+        c.start()
+        same_half.append(c)
+
+    def fwd_send(j):
+        return remote(v.at[h, j], v.at[h, j], s_f.at[j], r_f.at[j], (s, w, oh))
 
     zf_copy.wait()
     loads[3].wait()
 
-    def transform(yt):
+    def transform(yt, carry):
         rows = pl.ds(pl.multiple_of(yt * 8, 8), 8)
         zs = []
         for i in range(2):
@@ -165,12 +189,23 @@
             both = dot(hi, zf[...])
             zs.append(both[:, :CB] + (both[:, CB:] + dot(lo, zf[:, :CB])))
         res = const_dot(xf[0], xf[1], jnp.concatenate(zs, axis=1))
-        v[h, yt, 0] = res[:, :CB].reshape(NX, 8, CB)
-        v[h, yt, 1] = res[:, CB:].reshape(NX, 8, CB)
-
-    transform(0)
-    pl.semaphore_wait(barrier, 6)
-    fwd_send(0).start()
+        vt[yt, 0] = res[:, :CB].reshape(NX, 8, CB)
+        vt[yt, 1] = res[:, CB:].reshape(NX, 8, CB)
+        return carry
+
+    lax.fori_loop(0, 4, transform, 0)
+
+    def pack_nodes(i, carry):
+        at = pl.ds(pl.multiple_of(i * 8, 8), 8)
+        for arr in range(2):
+            got = regroup([vt[yt, arr, at] for yt in range(4)])
+            for j in range(4):
+                v[h, j, arr, at] = got[j]
+        return carry
+
+    lax.fori_loop(0, 4, pack_nodes, 0, unroll=True)
+    for j in range(3):
+        fwd_send(j).start()
 
     small = [
         remote(sycol.at[h], sycol.at[h], s_y, r_y, (s, w, oh)),
@@ -181,31 +216,6 @@
         small.append(remote(amp.at[w], amp.at[w], s_a.at[d], r_a.at[w], (s, other(d), h)))
     for c in small:
         c.start()
-    own_robin.wait()
-
-    def pack_robin(p, carry):
-        lanes = pl.ds(pl.multiple_of(p * CB, CB), CB)
-        for side in range(2):
-            got = regroup([rin[side, :, pl.ds(8 * q, 8), lanes] for q in range(4)])
-            for j in range(4):
-                rp[p, j, side] = got[j]
-        return carry
-
-    lax.fori_loop(0, TM, pack_robin, 0)
-    same_half = []
-    for d in range(1, TM):
-        c = remote(rp.at[other(d)], rb.at[h, :, w], s_rs.at[d], r_rb.at[w], (s, other(d), h))
-        c.start()
-        same_half.append(c)
-    keep_robin = pltpu.make_async_copy(rp.at[w], rb.at[h, :, w], s_rl.at[1])
-    keep_robin.start()
-
-    def fwd_chunk(yt, carry):
-        transform(yt)
-        fwd_send(yt).start()
-        return carry
-
-    lax.fori_loop(1, 4, fwd_chunk, 0)
 
     for c in loads[4:9]:
         c.wait()
@@ -246,41 +256,44 @@
 
     lax.fori_loop(0, NX, clear, 0)
 
-    for yt in range(4):
-        fwd_send(yt).wait_send()
     keep_robin.wait()
     for d in range(1, TM):
         f = other(d)
         remote(rb.at[h, :, f], rb.at[h, :, f], s_rs.at[d], r_rb.at[f], (s, f, h)).wait_recv()
         remote(amp.at[f], amp.at[f], s_a.at[d], r_a.at[f], (s, f, h)).wait_recv()
 
-    def cross(j):
-        return remote(rb.at[h, j], rb.at[h, j], s_ro.at[j], r_ro.at[j], (s, w, oh))
-
-    for j in range(2):
-        cross(j).start()
+    def cross(j, d):
+        part = rb.at[h, j, other(d)]
+        return remote(part, part, s_ro.at[j, d], r_ro.at[j, d], (s, w, oh))
+
+    def cross_start(j):
+        for d in range(1, TM):
+            cross(j, d).start()
+
     for c in loads[9:]:
         c.wait()
 
-    for yt in range(4):
-        remote(v.at[oh, yt], v.at[oh, yt], s_f.at[yt], r_f.at[yt], (s, w, oh)).wait_recv()
-
-    def y_forward(g, carry):
-        at = pl.ds(g * 4, 4)
-        rhs = jnp.concatenate([v[:, :, i, at].reshape(256, CB) for i in range(2)], axis=1)
-        res = const_dot(yf[0], yf[1], rhs)
-        both = res.reshape(8, 4, 8, 2 * CB)
-        for half in range(2):
-            tiles = both[4 * half:4 * half + 4]
-            got = regroup([tiles[q][:, :, :CB] for q in range(4)])
-            for j in range(4):
-                modes[0, j, half, at] = got[j]
-            got = regroup([tiles[q][:, :, CB:] for q in range(4)])
-            for j in range(4):
-                src[j, half, at] = got[j]
-        return carry
-
-    lax.fori_loop(0, 8, y_forward, 0)
+    def y_forward(j):
+        for i in range(2):
+            def at(n):
+                return pl.ds(16 * i + 4 * n, 4)
+
+            sides = []
+            for arr in range(2):
+                rows = []
+                for hh in range(2):
+                    rows += regroup([v[hh, j, arr, at(n)] for n in range(4)])
+                sides.append(jnp.concatenate([x.reshape(32, CB) for x in rows], axis=0))
+            res = const_dot(yf[0], yf[1], jnp.concatenate(sides, axis=1))
+            both = res.reshape(8, 4, 8, 2 * CB)
+            for half in range(2):
+                tiles = both[4 * half:4 * half + 4]
+                got = regroup([tiles[q][:, :, :CB] for q in range(4)])
+                for n in range(4):
+                    modes[0, j, half, at(n)] = got[n]
+                got = regroup([tiles[q][:, :, CB:] for q in range(4)])
+                for n in range(4):
+                    src[j, half, at(n)] = got[n]
 
     def steps(k, half, j, traces):
         for g in range(4):
@@ -310,46 +323,42 @@
                         e0, e1 = tr[t, 0], tr[t, 1]
                         o0 = tr[t, 2] + val
                         o1 = tr[t, 3] + slo
-                        ob[1, j, t] = coef[0] * (e1 + o1) + coef[1] * (e0 + o0)
-                        ob[0, j, t] = coef[3] * (e0 - o0) - coef[2] * (o1 - e1)
+                        ob[k, j, 1, t] = coef[0] * (e1 + o1) + coef[1] * (e0 + o0)
+                        ob[k, j, 0, t] = coef[3] * (e0 - o0) - coef[2] * (o1 - e1)
             for i in range(8):
                 modes[k + 1, j, half, a0 + i] = mu[i]
 
-    lanes = pl.ds(pl.multiple_of(w * CB, CB), CB)
-
-    def block(side, k):
-        return ob2.at[side, k]
-
-    def window_send(side, k):
-        return remote(block(side, k), st.at[side, :, :, lanes], s_1.at[side, k], r_1.at[side, w], (s, k, h))
-
-    def window_keep(side):
-        return pltpu.make_async_copy(block(side, w), st.at[side, :, :, lanes], s_1l.at[side])
-
-    def own_window(k, carry):
-        def own_steps(j, c):
+    def window_send(j, k):
+        return remote(ob.at[k, j], st1.at[w, j], s_1.at[j, k], r_1.at[j, w], (s, k, h))
+
+    def window_keep(j):
+        return pltpu.make_async_copy(ob.at[w, j], st1.at[w, j], s_1l.at[j])
+
+    def own_quarter(j, carry):
+        remote(v.at[oh, j], v.at[oh, j], s_f.at[j], r_f.at[j], (s, w, oh)).wait_recv()
+        fwd_send(j).wait_send()
+
+        @pl.when(j < 1)
+        def _():
+            fwd_send(j + 3).start()
+
+        @pl.when(j >= 1)
+        def _():
+            cross_start(j - 1)
+
+        y_forward(j)
+
+        def own_steps(k, c):
             steps(k, h, j, True)
             return c
 
-        lax.fori_loop(0, 4, own_steps, 0)
-        for side in range(2):
-            got = regroup([ob[side, j] for j in range(4)])
-            for q in range(4):
-                ob2[side, k, :, pl.ds(8 * q, 8), :] = got[q]
-
-        @pl.when(k != w)
-        def _():
-            window_send(0, k).start()
-            window_send(1, k).start()
-
-        @pl.when(k == w)
-        def _():
-            window_keep(0).start()
-            window_keep(1).start()
-
+        lax.fori_loop(0, TM, own_steps, 0)
+        for d in range(1, TM):
+            window_send(j, other(d)).start()
+        window_keep(j).start()
         return carry
 
-    lax.fori_loop(0, TM, own_window, 0)
+    lax.fori_loop(0, 4, own_quarter, 0)
 
     def end_send(j, k):
         return remote(ubuf.at[j, k], wr.at[j, w], s_w.at[j, k], r_w.at[j, w], (s, k, h))
@@ -363,26 +372,45 @@
             (left if side == 1 else right, w, h),
         )
 
-    def finish_robin():
-        for side in range(2):
-            window_keep(side).wait()
+    def unpack_robin():
+        for j in range(4):
+            window_keep(j).wait()
             for d in range(1, TM):
                 f = other(d)
-                to = st.at[side, :, :, pl.ds(pl.multiple_of(f * CB, CB), CB)]
-                remote(block(side, f), to, s_1.at[side, f], r_1.at[side, f], (s, f, h)).wait_recv()
-            robin_send(side).start()
+                remote(ob.at[f, j], st1.at[f, j], s_1.at[j, f], r_1.at[j, f], (s, f, h)).wait_recv()
+
+        def unpack(p, c):
+            lanes = pl.ds(pl.multiple_of(p * CB, CB), CB)
+            for side in range(2):
+                got = regroup([st1[p, j, side] for j in range(4)])
+                for q in range(4):
+                    st[side, :, pl.ds(8 * q, 8), lanes] = got[q]
+            return c
+
+        lax.fori_loop(0, TM, unpack, 0)
 
     def quarter(j, carry):
-        remote(rb.at[oh, j], rb.at[oh, j], s_ro.at[j], r_ro.at[j], (s, w, oh)).wait_recv()
-        cross(j).wait_send()
-
-        @pl.when(j < 2)
-        def _():
-            cross(j + 2).start()
+        for d in range(1, TM):
+            part = rb.at[oh, j, other(d)]
+            remote(part, part, s_ro.at[j, d], r_ro.at[j, d], (s, w, oh)).wait_recv()
+            cross(j, d).wait_send()
+
+        @pl.when(j == 0)
+        def _():
+            remote(rp.at[w], rb.at[oh, :, w], s_cw, r_cw, (s, w, oh)).wait_recv()
+
+        @pl.when(j < 1)
+        def _():
+            cross_start(j + 3)
+
+        @pl.when(j == 1)
+        def _():
+            unpack_robin()
 
         @pl.when(j == 3)
         def _():
-            finish_robin()
+            robin_send(0).start()
+            robin_send(1).start()
 
         def body(k, c):
             steps(k, oh, j, False)
@@ -408,7 +436,7 @@
             tbuf[:, pl.ds(g * 8 + 4, 4)] = res[:, CB:].reshape(4, 4, 8, CB)
             return c
 
-        lax.fori_loop(0, 4, y_inverse, 0)
+        lax.fori_loop(0, 4, y_inverse, 0, unroll=True)
 
         def x_inverse(q, c):
             rhs = jnp.concatenate(
@@ -419,7 +447,7 @@
             xbuf[2 * q + 1] = res[:, CB:].reshape(NX, 8, CB)
             return c
 
-        lax.fori_loop(0, 2, x_inverse, 0)
+        lax.fori_loop(0, 2, x_inverse, 0, unroll=True)
 
         def by_window(i, c):
             at = pl.ds(pl.multiple_of(i * 8, 8), 8)
@@ -428,7 +456,7 @@
                 ubuf[j, k, at] = got[k]
             return c
 
-        lax.fori_loop(0, 4, by_window, 0)
+        lax.fori_loop(0, 4, by_window, 0, unroll=True)
         for d in range(1, TM):
             end_send(j, other(d)).start()
         end_keep(j).start()
@@ -449,13 +477,12 @@
             at = pl.ds(pl.multiple_of(i * 8, 8), 8)
             got = regroup([wr[j, p, at] for p in range(TM)])
             hi, lo = split(jnp.concatenate([x.reshape(64, CB) for x in got], axis=0))
-            m_hi, m_lo = zi[0, j], zi[1, j]
-            part = dot(hi, m_hi) + (dot(lo, m_hi) + dot(hi, m_lo))
+            part = dot(jnp.concatenate([hi, lo], axis=1), zi[j, :2 * CB]) + dot(hi, zi[j, 2 * CB:])
             for yt in range(4):
                 ends_out[0, at, pl.ds(8 * yt, 8), :] += part[64 * yt:64 * yt + 64].reshape(8, 8, NZ)
             return c
 
-        lax.fori_loop(0, 4, body, 0)
+        lax.fori_loop(0, 4, body, 0, unroll=True)
 
     lax.fori_loop(0, 4, quarter, 0)
     z_inverse(3)
@@ -464,10 +491,10 @@
         c.wait_send()
     for c in same_half:
         c.wait_send()
+    cross_own.wait_send()
     for d in range(1, TM):
-        for side in range(2):
-            window_send(side, other(d)).wait_send()
         for j in range(4):
+            window_send(j, other(d)).wait_send()
             end_send(j, other(d)).wait_send()
     for side in range(2):
         robin_send(side).wait()
@@ -498,6 +525,7 @@
             pltpu.VMEM(xi.shape, BF16), pltpu.VMEM(zi.shape, BF16),
             pltpu.VMEM((2, NX, 32, NZ), F32),
             pltpu.VMEM((NZ, 2 * CB), BF16),
+            pltpu.VMEM((4, 2, NX) + tile, F32),
             pltpu.VMEM((2, 4, 2, NX) + tile, F32),
             pltpu.VMEM((2, 32, CB), F32),
             pltpu.VMEM((3,) + tile, F32),
@@ -510,16 +538,17 @@
             pltpu.VMEM((4, 2, NX) + tile, F32),
             pltpu.VMEM((STEPS, 4) + tile, F32),
             pltpu.VMEM((4,) + tile, F32),
-            pltpu.VMEM((2, 4, STEPS) + tile, F32),
-            pltpu.VMEM((2, TM, STEPS, 32, CB), F32),
+            pltpu.VMEM((TM, 4, 2, STEPS) + tile, F32),
+            pltpu.VMEM((TM, 4, 2, STEPS) + tile, F32),
             pltpu.VMEM((2, STEPS, 32, NZ), F32),
             pltpu.VMEM((4, NX) + tile, F32),
             pltpu.VMEM((4, NX) + tile, F32),
             pltpu.VMEM((4, TM, NX) + tile, F32),
             pltpu.VMEM((4, TM, NX) + tile, F32),
-            dma((13,)), dma((2, 4)), dma, dma((2,)), dma((TM,)), dma((TM,)), dma((4,)), dma((4,)),
+            dma((13,)), dma((2, 4)), dma, dma((2,)), dma((TM,)), dma((TM,)), dma, dma,
+            dma((4, TM)), dma((4, TM)),
             dma((4,)), dma((4,)), dma, dma, dma((2,)), dma((2,)), dma((TM,)), dma((TM,)),
-            dma((2, TM)), dma((2, TM)), dma((2,)), dma((2,)), dma((2,)),
+            dma((4, TM)), dma((4, TM)), dma((4,)), dma((2,)), dma((2,)),
             dma((4, TM)), dma((4, TM)), dma((4,)),
         ],
         compiler_params=pltpu.CompilerParams(

time: 88.1 us -> 82.6 us (0.938)
  the two profiles are of different devices: /device:TPU:7 before, /device:TPU:1 now
where the time goes in v5:
time: 82.6 us; the launch traced here: 82.5 us
  Pallas kernels  78.3 us (95%)
  local copies, waits for them, and re-layouts  2.29 us (3%)
  between operations  1.93 us (2%)
    pallas_call x1, Pallas kernels, local(): pl.pallas_call(sweep_kernel, out_shape=(pltpu.VMEM((1, 2, STEPS, 32, NZ),...  78.3 us
    unnamed x2, local copies, waits for them, and re-layouts  2.29 us

profile of v5, /device:TPU:1, one launch (start us, length us, event | category | flops | bytes accessed | tf_op | source)
XLA Modules:
  0.0 82.5 jit_solution(6298500654536333537)
XLA Ops:
  1.9 78.3 %sweep.1 = (f32[1,2,8,32,512]{4,3,2,1,0:T(8,128)S(1)}, f32[1,32,32,512]{3,2,1,0:T(8,128)S(1)}) custom-call(f32[32,32,512]{2,1,0:T(8,128)} %state_in.1, f32[32,32,512]{2,1,0:T(8,128)} %heat_in.1, f32[1,2,8,32,512]{4,3,2,1,0:T(8,128)} %robin_in.1, bf16[4,512,256]{2,1,0:T(8,128)(2,1)} %constant.16.clone.zf_in, f32[8]{0:T(128)} %amp_in.1, f32[1]{0:T(128)S(6)} %copy.23.diff_in, ...), custom_call_target="tpu_custom_call" | custom-call | tf_op jit(solution)/shard_map/sweep/pallas_call | solution.py:511
  80.2 1.0 %copy.21 = f32[1,2,8,32,512]{4,3,2,1,0:T(8,128)} copy(f32[1,2,8,32,512]{4,3,2,1,0:T(8,128)S(1)} %get-tuple-element.2) | data formatting | bytes 2097152
  81.2 1.3 %copy.22 = f32[1,32,32,512]{3,2,1,0:T(8,128)} copy(f32[1,32,32,512]{3,2,1,0:T(8,128)S(1)} %get-tuple-element.3) | data formatting | bytes 4194304

commit v6 on v5

--- a/solution.py
+++ b/solution.py
@@ -193,7 +193,7 @@
         vt[yt, 1] = res[:, CB:].reshape(NX, 8, CB)
         return carry
 
-    lax.fori_loop(0, 4, transform, 0)
+    lax.fori_loop(0, 4, transform, 0, unroll=True)
 
     def pack_nodes(i, carry):
         at = pl.ds(pl.multiple_of(i * 8, 8), 8)
@@ -369,7 +369,7 @@
     def robin_send(side):
         return remote(
             st.at[side], robin_out.at[0, side], s_o.at[side], r_o.at[side],
-            (left if side == 1 else right, w, h),
+            (jnp.where(side == 1, left, right), w, h),
         )
 
     def unpack_robin():
@@ -407,10 +407,9 @@
         def _():
             unpack_robin()
 
-        @pl.when(j == 3)
-        def _():
-            robin_send(0).start()
-            robin_send(1).start()
+        @pl.when(j >= 2)
+        def _():
+            robin_send(j - 2).start()
 
         def body(k, c):
             steps(k, oh, j, False)
@@ -461,13 +460,13 @@
             end_send(j, other(d)).start()
         end_keep(j).start()
 
-        @pl.when(j > 0)
-        def _():
-            z_inverse(j - 1)
+        @pl.when(j > 1)
+        def _():
+            z_inverse(j - 2, 0)
 
         return carry
 
-    def z_inverse(j):
+    def z_inverse(j, carry):
         end_keep(j).wait()
         for d in range(1, TM):
             f = other(d)
@@ -482,10 +481,10 @@
                 ends_out[0, at, pl.ds(8 * yt, 8), :] += part[64 * yt:64 * yt + 64].reshape(8, 8, NZ)
             return c
 
-        lax.fori_loop(0, 4, body, 0, unroll=True)
+        return lax.fori_loop(0, 4, body, carry, unroll=True)
 
     lax.fori_loop(0, 4, quarter, 0)
-    z_inverse(3)
+    lax.fori_loop(2, 4, z_inverse, 0)
 
     for c in small:
         c.wait_send()

time: 82.6 us -> 79.6 us (0.964)
  the two profiles are of different devices: /device:TPU:1 before, /device:TPU:120 now
where the time goes in v6:
time: 79.6 us; the launch traced here: 79.5 us
  Pallas kernels  75.3 us (95%)
  local copies, waits for them, and re-layouts  2.29 us (3%)
  between operations  1.93 us (2%)
    pallas_call x1, Pallas kernels, local(): pl.pallas_call(sweep_kernel, out_shape=(pltpu.VMEM((1, 2, STEPS, 32, NZ),...  75.3 us
    unnamed x2, local copies, waits for them, and re-layouts  2.29 us

profile of v6, /device:TPU:120, one launch (start us, length us, event | category | flops | bytes accessed | tf_op | source)
XLA Modules:
  0.0 79.5 jit_solution(8962579281927198559)
XLA Ops:
  1.9 75.3 %sweep.1 = (f32[1,2,8,32,512]{4,3,2,1,0:T(8,128)S(1)}, f32[1,32,32,512]{3,2,1,0:T(8,128)S(1)}) custom-call(f32[32,32,512]{2,1,0:T(8,128)} %state_in.1, f32[32,32,512]{2,1,0:T(8,128)} %heat_in.1, f32[1,2,8,32,512]{4,3,2,1,0:T(8,128)} %robin_in.1, bf16[4,512,256]{2,1,0:T(8,128)(2,1)} %constant.16.clone.zf_in, f32[8]{0:T(128)} %amp_in.1, f32[1]{0:T(128)S(6)} %copy.23.diff_in, ...), custom_call_target="tpu_custom_call" | custom-call | tf_op jit(solution)/shard_map/sweep/pallas_call | solution.py:510
  77.3 1.0 %copy.21 = f32[1,2,8,32,512]{4,3,2,1,0:T(8,128)} copy(f32[1,2,8,32,512]{4,3,2,1,0:T(8,128)S(1)} %get-tuple-element.2) | data formatting | bytes 2097152
  78.2 1.3 %copy.22 = f32[1,32,32,512]{3,2,1,0:T(8,128)} copy(f32[1,32,32,512]{3,2,1,0:T(8,128)S(1)} %get-tuple-element.3) | data formatting | bytes 4194304

commit v7 on v6

--- a/solution.py
+++ b/solution.py
@@ -455,9 +455,14 @@
                 ubuf[j, k, at] = got[k]
             return c
 
-        lax.fori_loop(0, 4, by_window, 0, unroll=True)
-        for d in range(1, TM):
-            end_send(j, other(d)).start()
+        for part in range(2):
+            lax.fori_loop(2 * part, 2 * part + 2, by_window, 0, unroll=True)
+            rows = pl.ds(16 * part, 16)
+            for d in range(1, TM):
+                k = other(d)
+                remote(
+                    ubuf.at[j, k, rows], wr.at[j, w, rows], s_w.at[j, k], r_w.at[j, w], (s, k, h)
+                ).start()
         end_keep(j).start()
 
         @pl.when(j > 1)

time: 79.6 us -> 79.6 us (level)
  no operation moved by 1% of the time
where the time goes in v7:
time: 79.6 us; the launch traced here: 79.5 us
  Pallas kernels  75.3 us (95%)
  local copies, waits for them, and re-layouts  2.29 us (3%)
  between operations  1.93 us (2%)
    pallas_call x1, Pallas kernels, local(): pl.pallas_call(sweep_kernel, out_shape=(pltpu.VMEM((1, 2, STEPS, 32, NZ),...  75.3 us
    unnamed x2, local copies, waits for them, and re-layouts  2.29 us

profile of v7, /device:TPU:120, one launch (start us, length us, event | category | flops | bytes accessed | tf_op | source)
XLA Modules:
  0.0 79.5 jit_solution(14409780345243888210)
XLA Ops:
  1.9 75.3 %sweep.1 = (f32[1,2,8,32,512]{4,3,2,1,0:T(8,128)S(1)}, f32[1,32,32,512]{3,2,1,0:T(8,128)S(1)}) custom-call(f32[32,32,512]{2,1,0:T(8,128)} %state_in.1, f32[32,32,512]{2,1,0:T(8,128)} %heat_in.1, f32[1,2,8,32,512]{4,3,2,1,0:T(8,128)} %robin_in.1, bf16[4,512,256]{2,1,0:T(8,128)(2,1)} %constant.16.clone.zf_in, f32[8]{0:T(128)} %amp_in.1, f32[1]{0:T(128)S(6)} %copy.23.diff_in, ...), custom_call_target="tpu_custom_call" | custom-call | tf_op jit(solution)/shard_map/sweep/pallas_call | solution.py:515
  77.2 1.0 %copy.21 = f32[1,2,8,32,512]{4,3,2,1,0:T(8,128)} copy(f32[1,2,8,32,512]{4,3,2,1,0:T(8,128)S(1)} %get-tuple-element.2) | data formatting | bytes 2097152
  78.2 1.3 %copy.22 = f32[1,32,32,512]{3,2,1,0:T(8,128)} copy(f32[1,32,32,512]{3,2,1,0:T(8,128)S(1)} %get-tuple-element.3) | data formatting | bytes 4194304
